TPU v7x, 32 devices: a whole 2x2x4 slice. The times are simulated.
32 devices in a mesh: lat: 4 (over y, x), lon: 8 (over z, core).
Axes of the slice: x: 2, y: 2, z: 4, core: 2. Of those that a mesh axis runs over, the one named last changes fastest.
Arguments:
- coarse_field: bfloat16 [1, 128, 128, 512], P(None, None, 'lat', 'lon'), may hold values from -6 to 6
- cotangent: bfloat16 [1, 64, 256, 1024], P(None, None, 'lat', 'lon'), may hold values from -6 to 6
- tconv_weight: bfloat16 [4, 64, 128], replicated, may hold values from -0.5 to 0.5
- conv_weight: bfloat16 [64, 576], replicated, may hold values from -0.25 to 0.25
Outputs:
- coarse_grad: bfloat16 [1, 128, 128, 512], P(None, None, 'lat', 'lon')
- tconv_grad: float32 [4, 64, 128], replicated
- conv_grad: float32 [64, 576], replicated
All inputs are finite; a program needn't handle non-finite values.
Results may differ from a plain program's by a relative error of at most 0.0049.
Values may be sent and summed in bfloat16 or wider, within the bound.
No kernel may reach another device: no remote copies, remote signals or barrier semaphores. Data moves between devices by JAX's collectives and lax.ppermute only.
A program may use at most 128 MiB of HBM per device.

v0:
```python
import functools
import math

import jax
import jax.numpy as jnp
from jax import lax
from jax.experimental import pallas as pl
from jax.experimental.pallas import tpu as pltpu
from jax.sharding import PartitionSpec as P

F32, BF16 = jnp.float32, jnp.bfloat16
AXES = ("lat", "lon")
SHIFTS = (-1, 0, 1, 2)
VMEM = pl.BlockSpec(memory_space=pltpu.VMEM)
SMEM = pl.BlockSpec(memory_space=pltpu.SMEM)


def product(lhs, rhs, lhs_dim, rhs_dim):
    dims = (((lhs_dim,), (rhs_dim,)), ((), ()))
    return lax.dot_general(lhs, rhs, dims, preferred_element_type=F32)


def gather_kernel(flags, cot, recv_a, recv_b, near, send_a, send_b, wide, edges):
    channels, rows, cols = cot.shape
    half = cols // 2
    pairs = near.shape[0]
    north_is_a = flags[0] == 1

    def widen(o, carry):
        start = pl.multiple_of(o * rows, rows)
        wide[pl.ds(start, rows), :] = cot[o].astype(F32)
        return carry

    lax.fori_loop(0, channels, widen, 0, unroll=4)
    row_id = lax.broadcasted_iota(jnp.int32, (4 * half, cols), 0)
    col_id = lax.broadcasted_iota(jnp.int32, (4 * half, cols), 1)
    shift = row_id // half - 1
    pick = jnp.where(col_id == 2 * (row_id % half) + shift, 1.0, 0.0).astype(BF16)
    from_a = recv_a[...].astype(F32)
    from_b = recv_b[...].astype(F32)
    top = jnp.where(north_is_a, from_a, from_b).astype(BF16)
    bottom = jnp.where(north_is_a, from_b, from_a).astype(BF16)

    def row(r):
        return wide[pl.ds(r, channels, stride=rows), :].astype(BF16)

    def emit(m, parts):
        out = product(pick, jnp.concatenate(parts, axis=0), 1, 1)
        for k in range(len(parts) // 2):
            block = out[:, k * 2 * channels : (k + 1) * 2 * channels]
            near[m + k] = block.astype(BF16)
            edges[0, pl.ds(m + k, 1), :] = block[half : half + 1]
            edges[1, pl.ds(m + k, 1), :] = block[3 * half - 1 : 3 * half]

    emit(0, [top, row(0)])

    def middle(q, carry):
        m = 1 + 2 * q
        emit(m, [row(2 * m - 1), row(2 * m), row(2 * m + 1), row(2 * m + 2)])
        return carry

    lax.fori_loop(0, (pairs - 3) // 2, middle, 0)
    emit(pairs - 2, [row(rows - 3), row(rows - 2), row(rows - 1), bottom])
    odd = flags[1] == 1
    send_a[...] = jnp.where(odd, edges[0], edges[1]).astype(BF16)
    send_b[...] = jnp.where(odd, edges[1], edges[0]).astype(BF16)


def main_kernel(flags, x, near_in, recv_a, recv_b, up_w, conv_w, grad, sums,
                near, polar, rims, weights, conv_acc, up_acc, feature, sem):
    channels = conv_w.shape[0]
    pairs, quad, lanes = near.shape
    half = quad // 4
    rows = pairs - 1
    group = 4
    cells = group * half
    steps = rows // group
    load = pltpu.make_async_copy(near_in, near, sem)
    load.start()
    weights[...] = jnp.zeros_like(weights)
    for d in range(4):
        for e in range(4):
            for p in range(2):
                for q in range(2):
                    a, b = p - SHIFTS[e], q - SHIFTS[d]
                    if abs(a) <= 1 and abs(b) <= 1:
                        tap = 3 * (a + 1) + b + 1
                        weights[
                            d,
                            e * channels : (e + 1) * channels,
                            (2 * p + q) * channels : (2 * p + q + 1) * channels,
                        ] = conv_w[:, tap * channels : (tap + 1) * channels]
    conv_acc[...] = jnp.zeros_like(conv_acc)
    up_acc[...] = jnp.zeros_like(up_acc)
    odd = flags[1] == 1
    from_a = recv_a[...].astype(F32)
    from_b = recv_b[...].astype(F32)
    rims[0] = jnp.where(odd, from_a, from_b)
    rims[1] = jnp.where(odd, from_b, from_a)
    load.wait()
    tile = 16
    tile_row = lax.broadcasted_iota(jnp.int32, (tile, lanes), 0)

    def set_rims(m, carry):
        west = near[m, 0:tile, :].astype(F32)
        near[m, 0:tile, :] = jnp.where(
            tile_row == 0, rims[0, pl.ds(m, 1), :], west
        ).astype(BF16)
        east = near[m, quad - tile : quad, :].astype(F32)
        near[m, quad - tile : quad, :] = jnp.where(
            tile_row == tile - 1, rims[1, pl.ds(m, 1), :], east
        ).astype(BF16)
        return carry

    lax.fori_loop(0, pairs, set_rims, 0, unroll=3)
    lane_id = lax.broadcasted_iota(jnp.int32, (quad, lanes), 1)
    at_north = flags[2] == 1
    at_south = flags[3] == 1

    @pl.when(at_north)
    def _():
        block = near[0].astype(F32)
        polar[0] = jnp.where(lane_id < channels, block, 0.0).astype(BF16)
        near[0] = jnp.where(lane_id < channels, 0.0, block).astype(BF16)

    @pl.when(at_south)
    def _():
        block = near[pairs - 1].astype(F32)
        polar[1] = jnp.where(lane_id < channels, 0.0, block).astype(BF16)
        near[pairs - 1] = jnp.where(lane_id < channels, block, 0.0).astype(BF16)

    def step(s, carry):
        first = s * group
        start = pl.multiple_of(s * cells, cells)
        coarse = x[pl.ds(start, cells), :]
        up = product(coarse, up_w[...], 1, 1)
        gate = 1.0 / (1.0 + jnp.exp(-up))
        active = (up * gate).astype(BF16)
        slope = gate * (1.0 + up * (1.0 - gate))
        active_t = active.T
        total = None
        for d in range(4):
            lower = near[pl.ds(first, group), d * half : (d + 1) * half, :]
            upper = near[pl.ds(first + 1, group), d * half : (d + 1) * half, :]
            around = jnp.concatenate(
                [lower.reshape(cells, lanes), upper.reshape(cells, lanes)], axis=1
            )
            term = product(around, weights[d], 1, 0)
            total = term if total is None else total + term
            conv_acc[d] += product(active_t, around, 1, 0)
        feature[...] = total

        @pl.when(jnp.logical_and(s == 0, at_north))
        def _():
            for d in range(4):
                cap = polar[0, d * half : (d + 1) * half, :]
                feature[0:half, 0:lanes] += product(cap, weights[d, lanes : 2 * lanes, 0:lanes], 1, 0)
                conv_acc[d, 0:lanes, lanes : 2 * lanes] += product(
                    active[0:half, 0:lanes], cap, 0, 0
                )

        @pl.when(jnp.logical_and(s == steps - 1, at_south))
        def _():
            for d in range(4):
                cap = polar[1, d * half : (d + 1) * half, :]
                feature[cells - half : cells, lanes : 2 * lanes] += product(
                    cap, weights[d, 0:lanes, lanes : 2 * lanes], 1, 0
                )
                conv_acc[d, lanes : 2 * lanes, 0:lanes] += product(
                    active[cells - half : cells, lanes : 2 * lanes], cap, 0, 0
                )

        pre = (feature[...] * slope).astype(BF16)
        grad[pl.ds(start, cells), :] = product(pre, up_w[...], 1, 0).astype(BF16)
        up_acc[...] += product(pre, coarse, 0, 0)
        return carry

    lax.fori_loop(0, steps, step, 0)
    fine = up_acc.shape[0]
    sums[0:fine, :] = up_acc[...]
    zero = jnp.zeros((channels, channels), F32)

    def tap_sum(tap):
        if tap > 8:
            return zero
        a, b = tap // 3 - 1, tap % 3 - 1
        total = None
        for p in range(2):
            for q in range(2):
                e, d = p - a + 1, q - b + 1
                part = conv_acc[
                    d,
                    (2 * p + q) * channels : (2 * p + q + 1) * channels,
                    e * channels : (e + 1) * channels,
                ]
                total = part if total is None else total + part
        return total

    for u in range(5):
        for k in range(2):
            feature[k * channels : (k + 1) * channels, 0:channels] = tap_sum(2 * u + k)
        block = feature[0 : 2 * channels, 0 : 2 * channels].T
        sums[fine + u * channels : fine + (u + 1) * channels, :] = block[0:channels]


def summed_everywhere(part, scale):
    members = lax.axis_size(AXES)
    rows, lanes = part.shape
    piece = -(-rows // members)
    if members * piece > rows:
        part = jnp.pad(part, ((0, members * piece - rows), (0, 0)))
    parts = lax.all_to_all(part.reshape(members, piece * lanes), AXES, 0, 0, tiled=True)
    own = jnp.sum(parts, axis=0) * scale
    spread = jnp.broadcast_to(own[None], (members, piece * lanes))
    whole = lax.all_to_all(spread, AXES, 0, 0, tiled=True)
    return whole.reshape(members * piece, lanes)[:rows]


def row_routes(lats, lons):
    half = lons // 2
    there = []
    for lat in range(lats):
        for lon in range(lons):
            if lon < half:
                target = (lat + 1, lon) if lat + 1 < lats else (lat, lon + half)
            else:
                target = (lat - 1, lon) if lat > 0 else (lat, lon - half)
            there.append((lat * lons + lon, target[0] * lons + target[1]))
    return there, [(b, a) for a, b in there]


def per_device(coarse_field, cotangent, tconv_weight, conv_weight):
    batch, channels, rows, cols = cotangent.shape
    in_channels = coarse_field.shape[1]
    lats, lons = lax.axis_size("lat"), lax.axis_size("lon")
    lat, lon = lax.axis_index("lat"), lax.axis_index("lon")
    assert batch == 1 and lons % 2 == 0
    coarse_rows, half = rows // 2, cols // 2
    cells = coarse_rows * half
    pairs = coarse_rows + 1
    fine = 4 * channels
    lanes = 2 * channels
    scale = 1.0 / math.sqrt(batch * rows * cols * lats * lons)
    first_half = lon < lons // 2
    flags = jnp.stack(
        [first_half, lon % 2 == 1, lat == 0, lat == lats - 1]
    ).astype(jnp.int32)

    cot = cotangent.reshape(channels, rows, cols)
    x = coarse_field.transpose(0, 2, 3, 1).reshape(cells, in_channels)
    up_w = tconv_weight.reshape(fine, in_channels)

    top, bottom = cot[:, 0], cot[:, rows - 1]
    there, back = row_routes(lats, lons)
    row_a = lax.ppermute(jnp.where(first_half, bottom, top), AXES, there)
    row_b = lax.ppermute(jnp.where(first_half, top, bottom), AXES, back)

    near, send_a, send_b = pl.pallas_call(
        gather_kernel,
        out_shape=(
            jax.ShapeDtypeStruct((pairs, 4 * half, lanes), BF16),
            jax.ShapeDtypeStruct((pairs, lanes), BF16),
            jax.ShapeDtypeStruct((pairs, lanes), BF16),
        ),
        in_specs=[SMEM, VMEM, VMEM, VMEM],
        out_specs=(VMEM, VMEM, VMEM),
        scratch_shapes=[
            pltpu.VMEM((channels * rows, cols), F32),
            pltpu.VMEM((2, pairs, lanes), F32),
        ],
        name="gather_rows",
    )(flags, cot, row_a, row_b)

    inner = [(i, i ^ 1) for i in range(lons)]
    outer = [(i, (i + (1 if i % 2 else -1)) % lons) for i in range(lons)]
    col_a = lax.ppermute(send_a, "lon", inner)
    col_b = lax.ppermute(send_b, "lon", outer)

    grad, sums = pl.pallas_call(
        main_kernel,
        out_shape=(
            jax.ShapeDtypeStruct((cells, in_channels), BF16),
            jax.ShapeDtypeStruct((fine + 5 * channels, lanes), F32),
        ),
        in_specs=[SMEM, VMEM, pl.BlockSpec(memory_space=pl.ANY), VMEM, VMEM, VMEM, VMEM],
        out_specs=(VMEM, VMEM),
        scratch_shapes=[
            pltpu.VMEM((pairs, 4 * half, lanes), BF16),
            pltpu.VMEM((2, 4 * half, lanes), BF16),
            pltpu.VMEM((2, pairs, lanes), F32),
            pltpu.VMEM((4, fine, fine), BF16),
            pltpu.VMEM((4, fine, fine), F32),
            pltpu.VMEM((fine, in_channels), F32),
            pltpu.VMEM((4 * half, fine), F32),
            pltpu.SemaphoreType.DMA,
        ],
        name="section",
    )(flags, x, near, col_a, col_b, up_w, conv_weight)

    whole = summed_everywhere(sums, scale)
    tconv_grad = whole[:fine].reshape(4, channels, in_channels)
    blocks = whole[fine:].reshape(5, channels, lanes)
    conv_grad = jnp.concatenate([blocks[u] for u in range(5)], axis=1)[:, : 9 * channels]
    coarse_grad = grad.reshape(1, coarse_rows, half, in_channels).transpose(0, 3, 1, 2)
    return (coarse_grad, tconv_grad, conv_grad)


def solution(mesh):
    return jax.shard_map(
        per_device,
        mesh=mesh,
        in_specs=(P(None, None, "lat", "lon"), P(None, None, "lat", "lon"), P(), P()),
        out_specs=(P(None, None, "lat", "lon"), P(), P()),
        check_vma=False,
    )
```

profile of v0, /device:TPU:0, one launch (start us, length us, event | category | flops | bytes accessed | tf_op | source)
XLA Modules:
  0.0 66.5 jit_solution(7636511710072555077)
XLA Ops:
  0.6 1.9 %copy.14 = bf16[1,64,64,128]{3,1,2,0:T(8,128)(2,1)S(1)} copy(bf16[1,64,64,128]{3,2,1,0:T(8,128)(2,1)} %param.5) | data formatting | bytes 2097152 | tf_op args[1]
  2.6 4.1 %collective-permute-start.1 = (bf16[64,128]{1,0:T(8,128)(2,1)S(1)}, bf16[64,128]{1,0:T(8,128)(2,1)S(1)}, u32[]{:S(2)}, u32[]{:S(2)}) collective-permute-start(bf16[64,128]{1,0:T(8,128)(2,1)S(1)} %get-tuple-element.13), channel_id=1, source_target_pairs={{8,0},{9,1},{10,2},{11,3},{0,4},{1,5},{2,6},{3,7},{16,8},{17,9},{1... | collective-permute-start | bytes 49160 | tf_op jit(solution)/shard_map/ppermute | solution.py:256
  6.7 0.0 collective-permute-start
  6.7 0.6 add_convert_fusion.flags
  7.3 0.8 %collective-permute-done.1.recv_b = bf16[64,128]{1,0:T(8,128)(2,1)S(1)} collective-permute-done((bf16[64,128]{1,0:T(8,128)(2,1)S(1)}, bf16[64,128]{1,0:T(8,128)(2,1)S(1)}, u32[]{:S(2)}, u32[]{:S(2)}) %collective-permute-start.1) | collective-permute-done | bytes 16416 | tf_op jit(solution)/shard_map/ppermute | solution.py:256
  8.1 0.0 copy-start
  8.1 3.2 %collective-permute-done.recv_a = bf16[64,128]{1,0:T(8,128)(2,1)S(1)} collective-permute-done((bf16[64,128]{1,0:T(8,128)(2,1)S(1)}, bf16[64,128]{1,0:T(8,128)(2,1)S(1)}, u32[]{:S(2)}, u32[]{:S(2)}) %collective-permute-start) | collective-permute-done | bytes 16416 | tf_op jit(solution)/shard_map/ppermute | solution.py:255
  11.3 0.0 copy-start.1
  11.3 0.0 copy-done
  11.3 0.6 copy-done.1
  11.9 6.7 %gather_rows.1 = (bf16[33,256,128]{2,1,0:T(8,128)(2,1)}, bf16[33,128]{1,0:T(8,128)(2,1)}, bf16[33,128]{1,0:T(8,128)(2,1)}) custom-call(s32[4]{0:T(128)} %add_convert_fusion.flags, bf16[64,64,128]{2,1,0:T(8,128)(2,1)} %bitcast.23, bf16[64,128]{1,0:T(8,128)(2,1)} %copy-done.1, bf16[64,128]{1,0:T(8,128)(2,1)} %copy-done), custom_call_target="tpu_custom_call" | custom-call | tf_op jit(solution)/shard_map/gather_rows/pallas_call | solution.py:258
  18.6 0.0 collective-permute-start.2
  18.6 1.7 %collective-permute-start.3 = (bf16[33,128]{1,0:T(8,128)(2,1)}, bf16[33,128]{1,0:T(8,128)(2,1)S(1)}, u32[]{:S(2)}, u32[]{:S(2)}) collective-permute-start(bf16[33,128]{1,0:T(8,128)(2,1)} %get-tuple-element.10), channel_id=1, source_target_pairs={{0,7},{1,2},{2,1},{3,4},{4,3},{5,6},{6,5},{7,0},{8,15},{9,10},{10,... | collective-permute-start | bytes 25352 | tf_op jit(solution)/shard_map/ppermute | solution.py:277
  20.3 0.0 collective-permute-done.2.recv_a
  20.3 0.0 copy-start.2
  20.3 3.4 %collective-permute-done.3.recv_b = bf16[33,128]{1,0:T(8,128)(2,1)S(1)} collective-permute-done((bf16[33,128]{1,0:T(8,128)(2,1)}, bf16[33,128]{1,0:T(8,128)(2,1)S(1)}, u32[]{:S(2)}, u32[]{:S(2)}) %collective-permute-start.3) | collective-permute-done | bytes 8480 | tf_op jit(solution)/shard_map/ppermute | solution.py:277
  23.7 0.0 copy-start.3
  23.7 0.0 copy-done.2
  23.7 0.6 copy-done.3
  24.3 11.9 %section.1 = (bf16[2048,128]{1,0:T(8,128)(2,1)}, f32[576,128]{1,0:T(8,128)}) custom-call(s32[4]{0:T(128)} %add_convert_fusion.flags, bf16[2048,128]{1,0:T(8,128)(2,1)} %bitcast.31, bf16[33,256,128]{2,1,0:T(8,128)(2,1)} %get-tuple-element.8.near_in, bf16[33,128]{1,0:T(8,128)(2,1)} %copy-done.2, bf16[33,128]{1,0:T(8,128)(2,1)} %copy-done.3, ...), custom_call_target="tpu_custom_call" | custom-call | tf_op jit(solution)/shard_map/section/pallas_call | solution.py:279
  36.3 15.1 %all_to_all.15 = f32[32,1,2304]{2,1,0:T(1,128)S(1)} all-to-all(f32[32,1,2304]{2,1,0:T(1,128)} %bitcast.32), channel_id=1, replica_groups=mesh['lat'=4,'lon'=8] {'lat','lon'}, dimensions={0} | all-to-all | bytes 589824 | tf_op jit(solution)/shard_map/all_to_all | solution.py:212
  51.4 0.2 reduce_sum.9
  51.6 0.2 broadcast_in_dim.2
  51.7 13.4 %all_to_all.16 = f32[32,1,2304]{2,1,0:T(1,128)S(1)} all-to-all(f32[32,1,2304]{2,1,0:T(1,128)S(1)} %broadcast_in_dim.2), channel_id=1, replica_groups=mesh['lat'=4,'lon'=8] {'lat','lon'}, dimensions={0} | all-to-all | bytes 589824 | tf_op jit(solution)/shard_map/all_to_all | solution.py:215
  65.1 0.7 slice.49
  65.8 0.0 copy-start.4
  65.8 0.7 copy-done.4
  (7 shorter events, 0.0 us)
Async XLA Ops:
  2.6 5.6 %collective-permute-start.1 = (bf16[64,128]{1,0:T(8,128)(2,1)S(1)}, bf16[64,128]{1,0:T(8,128)(2,1)S(1)}, u32[]{:S(2)}, u32[]{:S(2)}) collective-permute-start(bf16[64,128]{1,0:T(8,128)(2,1)S(1)} %get-tuple-element.13), channel_id=1, source_target_pairs={{8,0},{9,1},{10,2},{11,3},{0,4},{1,5},{2,6},{3,7},{16,8},{17,9},{1... | collective-permute-start | bytes 49160 | tf_op jit(solution)/shard_map/ppermute | solution.py:256
  6.7 4.6 %collective-permute-start = (bf16[64,128]{1,0:T(8,128)(2,1)S(1)}, bf16[64,128]{1,0:T(8,128)(2,1)S(1)}, u32[]{:S(2)}, u32[]{:S(2)}) collective-permute-start(bf16[64,128]{1,0:T(8,128)(2,1)S(1)} %get-tuple-element.14), channel_id=1, source_target_pairs={{0,8},{1,9},{2,10},{3,11},{4,0},{5,1},{6,2},{7,3},{8,16},{9,17},{1... | collective-permute-start | bytes 49160 | tf_op jit(solution)/shard_map/ppermute | solution.py:255
  8.1 3.2 %copy-start = (bf16[64,128]{1,0:T(8,128)(2,1)}, bf16[64,128]{1,0:T(8,128)(2,1)S(1)}, u32[]{:S(2)}) copy-start(bf16[64,128]{1,0:T(8,128)(2,1)S(1)} %collective-permute-done.1.recv_b) | copy-start | bytes 49156
  11.3 0.6 copy-start.1
  18.6 1.7 %collective-permute-start.2 = (bf16[33,128]{1,0:T(8,128)(2,1)}, bf16[33,128]{1,0:T(8,128)(2,1)S(1)}, u32[]{:S(2)}, u32[]{:S(2)}) collective-permute-start(bf16[33,128]{1,0:T(8,128)(2,1)} %get-tuple-element.9), channel_id=1, source_target_pairs={{0,1},{1,0},{2,3},{3,2},{4,5},{5,4},{6,7},{7,6},{8,9},{9,8},{10,11... | collective-permute-start | bytes 25352 | tf_op jit(solution)/shard_map/ppermute | solution.py:276
  18.6 5.1 %collective-permute-start.3 = (bf16[33,128]{1,0:T(8,128)(2,1)}, bf16[33,128]{1,0:T(8,128)(2,1)S(1)}, u32[]{:S(2)}, u32[]{:S(2)}) collective-permute-start(bf16[33,128]{1,0:T(8,128)(2,1)} %get-tuple-element.10), channel_id=1, source_target_pairs={{0,7},{1,2},{2,1},{3,4},{4,3},{5,6},{6,5},{7,0},{8,15},{9,10},{10,... | collective-permute-start | bytes 25352 | tf_op jit(solution)/shard_map/ppermute | solution.py:277
  20.3 3.4 %copy-start.2 = (bf16[33,128]{1,0:T(8,128)(2,1)}, bf16[33,128]{1,0:T(8,128)(2,1)S(1)}, u32[]{:S(2)}) copy-start(bf16[33,128]{1,0:T(8,128)(2,1)S(1)} %collective-permute-done.2.recv_a) | copy-start | bytes 25348
  23.7 0.6 copy-start.3
  65.8 0.7 %copy-start.4 = (f32[64,640]{1,0:T(8,128)}, f32[64,640]{1,0:T(8,128)S(1)}, u32[]{:S(2)}) copy-start(f32[64,640]{1,0:T(8,128)S(1)} %slice_dynamic-update-slice_fusion) | copy-start | bytes 491524
where the time goes:
time: 66.8 us; the launch traced here: 66.5 us
  blocking collectives  28.5 us (43%)
  Pallas kernels  18.6 us (28%)
  waiting for transfers between devices  7.43 us (11%)
  starting transfers between devices  5.84 us (9%)
  local copies, waits for them, and re-layouts  4.61 us (7%)
  other arithmetic  0.79 us (1%)
  between operations  0.71 us (1%)
    all_to_all x1, blocking collectives, summed_everywhere(): lax.all_to_all(part.reshape(members, piece * lanes), AXES, 0, 0, tiled=True)  15.1 us
    all_to_all x1, blocking collectives, summed_everywhere(): whole = lax.all_to_all(spread, AXES, 0, 0, tiled=True)  13.4 us
    pallas_call x1, Pallas kernels, per_device(): pl.pallas_call(main_kernel, out_shape=(jax.ShapeDtypeStruct((cells, in_ch...  11.9 us
    pallas_call x1, Pallas kernels, per_device(): pl.pallas_call(gather_kernel, out_shape=(jax.ShapeDtypeStruct((pairs, 4 *...  6.69 us
    ppermute x1, starting transfers between devices, per_device(): row_b = lax.ppermute(jnp.where(first_half, top, bottom), AXES, back)  4.12 us
    unnamed x15, local copies, waits for them, and re-layouts  3.79 us
    ppermute x1, waiting for transfers between devices, per_device(): col_b = lax.ppermute(send_b, 'lon', outer)  3.39 us
    ppermute x1, waiting for transfers between devices, per_device(): row_a = lax.ppermute(jnp.where(first_half, bottom, top), AXES, there)  3.19 us
  transfers between devices with their start and end apart: 4, of which 3 were waited for; matrix products, arithmetic and copies ran while one was open for 1% of the time, Pallas kernels for 0%

commit v1 on v0

v1 whole, which is shorter than its diff:
```python
import math

import jax
import jax.numpy as jnp
from jax import lax
from jax.experimental import pallas as pl
from jax.experimental.pallas import tpu as pltpu
from jax.sharding import PartitionSpec as P

F32, BF16 = jnp.float32, jnp.bfloat16
AXES = ("lat", "lon")
SHIFTS = (-1, 0, 1, 2)
VMEM = pl.BlockSpec(memory_space=pltpu.VMEM)
LIMIT = pltpu.CompilerParams(vmem_limit_bytes=24 * 2**20)


def product(lhs, rhs, lhs_dim, rhs_dim):
    dims = (((lhs_dim,), (rhs_dim,)), ((), ()))
    return lax.dot_general(lhs, rhs, dims, preferred_element_type=F32)


def resident(array):
    return pltpu.with_memory_space_constraint(array, pltpu.VMEM)


def place_weights(conv_w, weights, packed):
    channels, width = conv_w.shape
    pair = 2 * channels
    packed[0, :, 0:width] = conv_w[...]
    packed[1, :, 0 : width - channels] = conv_w[:, channels:width]
    weights[...] = jnp.zeros_like(weights)
    for e in range(4):
        for p in range(2):
            a = p - SHIFTS[e]
            if abs(a) > 1:
                continue
            tap = 3 * (a + 1)
            rows = slice(e * channels, (e + 1) * channels)
            low = p * pair
            for d in range(4):
                first = tap - SHIFTS[d] + 1
                if d == 0:
                    base = packed[first % 2, :, (first - first % 2) * channels :][:, 0:channels]
                    weights[d, rows, low : low + channels] = base
                elif d == 3:
                    weights[d, rows, low + channels : low + pair] = conv_w[
                        :, tap * channels : (tap + 1) * channels
                    ]
                else:
                    start = (first - first % 2) * channels
                    weights[d, rows, low : low + pair] = packed[
                        first % 2, :, start : start + pair
                    ]


def up_kernel(x, up_w, conv_w, slope, act_t, act_rim, weights, packed):
    fine = up_w.shape[0]
    rows = act_rim.shape[1]
    half = x.shape[0] // rows
    group = math.gcd(rows, 8)
    cells = group * half
    place_weights(conv_w, weights, packed)

    def step(s, carry):
        start = pl.multiple_of(s * cells, cells)
        up = product(x[pl.ds(start, cells), :], up_w[...], 1, 1)
        gate = 1.0 / (1.0 + jnp.exp(-up))
        active = up * gate
        slope[pl.ds(start, cells), :] = gate * (1.0 + up * (1.0 - gate))
        act_t[:, pl.ds(start, cells)] = active.astype(BF16).T
        for k in range(group):
            at = pl.ds(s * group + k, 1)
            act_rim[0, at, :] = active[k * half : k * half + 1]
            act_rim[1, at, :] = active[(k + 1) * half - 1 : (k + 1) * half]
        return carry

    lax.fori_loop(0, rows // group, step, 0)


def gather_kernel(cot, recv_a, recv_b, after, near, polar, send_a, send_b, edges):
    rows, channels, cols = cot.shape
    half = cols // 2
    pairs = near.shape[0]
    first_half = 2 * lax.axis_index("lon") < lax.axis_size("lon")
    odd = lax.rem(lax.axis_index("lon"), 2) == 1
    at_north = lax.axis_index("lat") == 0
    at_south = lax.axis_index("lat") == lax.axis_size("lat") - 1
    row_id = lax.broadcasted_iota(jnp.int32, (4 * half, cols), 0)
    col_id = lax.broadcasted_iota(jnp.int32, (4 * half, cols), 1)
    pick = jnp.where(col_id == 2 * (row_id % half) + row_id // half - 1, 1.0, 0.0)
    pick = pick.astype(BF16)
    from_a = recv_a[...].astype(F32)
    from_b = recv_b[...].astype(F32)
    top = jnp.where(first_half, from_a, from_b).astype(BF16)
    bottom = jnp.where(first_half, from_b, from_a).astype(BF16)

    def keep_edges(m, block):
        edges[0, pl.ds(m, 1), :] = block[half : half + 1]
        edges[1, pl.ds(m, 1), :] = block[3 * half - 1 : 3 * half]

    def middle(q, carry):
        m = 1 + 2 * q
        four = cot[pl.ds(2 * m - 1, 4)].reshape(4 * channels, cols)
        out = product(pick, four, 1, 1)
        for k in range(2):
            block = out[:, k * 2 * channels : (k + 1) * 2 * channels]
            near[m + k] = block.astype(BF16)
            keep_edges(m + k, block)
        return carry

    lane_id = lax.broadcasted_iota(jnp.int32, (4 * half, 2 * channels), 1)
    ends = ((0, top, cot[0], at_north), (pairs - 1, cot[rows - 1], bottom, at_south))
    for side, (m, one, two, pole) in enumerate(ends):
        block = product(pick, jnp.concatenate([one, two], axis=0), 1, 1)
        keep_edges(m, block)
        beyond = (lane_id < channels) if side == 0 else (lane_id >= channels)
        away = jnp.where(jnp.logical_and(beyond, pole), block, 0.0)
        polar[side] = away.astype(BF16)
        near[m] = (block - away).astype(BF16)
    lax.fori_loop(0, (pairs - 3) // 2, middle, 0, unroll=3)
    m = pairs - 2
    block = product(pick, cot[2 * m - 1 : 2 * m + 1].reshape(2 * channels, cols), 1, 1)
    near[m] = block.astype(BF16)
    keep_edges(m, block)
    send_a[...] = jnp.where(odd, edges[0], edges[1]).astype(BF16)
    send_b[...] = jnp.where(odd, edges[1], edges[0]).astype(BF16)


def spread_kernel(near, polar, act_t, weights, feature, conv_acc):
    pairs, quad, lanes = near.shape
    half, rows, fine = quad // 4, pairs - 1, weights.shape[1]
    group = math.gcd(rows, 8)
    cells = group * half
    all_w = weights[...].reshape(4 * fine, fine)

    def around(first, count, d):
        piece = slice(d * half, (d + 1) * half)
        lower = near[pl.ds(first, count), piece, :].reshape(count * half, lanes)
        upper = near[pl.ds(first + 1, count), piece, :].reshape(count * half, lanes)
        return [lower, upper]

    def step(s, carry):
        parts = []
        for d in range(4):
            parts += around(s * group, group, d)
        start = pl.multiple_of(s * cells, cells)
        feature[pl.ds(start, cells), :] = product(jnp.concatenate(parts, axis=1), all_w, 1, 0)
        return carry

    lax.fori_loop(0, rows // group, step, 0)
    for d in range(4):
        conv_acc[d] = product(act_t[...], jnp.concatenate(around(0, rows, d), axis=1), 1, 0)

    @pl.when(lax.axis_index("lat") == 0)
    def _():
        for d in range(4):
            cap = polar[0, d * half : (d + 1) * half, :]
            feature[0:half, 0:lanes] += product(cap, weights[d, lanes:fine, 0:lanes], 1, 0)
            conv_acc[d, 0:lanes, lanes:fine] += product(act_t[0:lanes, 0:half], cap, 1, 0)

    @pl.when(lax.axis_index("lat") == lax.axis_size("lat") - 1)
    def _():
        last = rows * half
        for d in range(4):
            cap = polar[1, d * half : (d + 1) * half, :]
            feature[last - half : last, lanes:fine] += product(
                cap, weights[d, 0:lanes, lanes:fine], 1, 0
            )
            padded = jnp.concatenate([jnp.zeros_like(cap), cap], axis=0)
            conv_acc[d, lanes:fine, 0:lanes] += product(
                act_t[lanes:fine, last - 2 * half : last], padded, 1, 0
            )


def finish_kernel(x, feature, slope, conv_acc, act_rim, col_a, col_b, weights, up_w,
                  grad, sums, extra, rims, rim_feature, rim_conv, up_acc):
    rows = act_rim.shape[1]
    fine, lanes = weights.shape[1], rims.shape[2]
    channels = lanes // 2
    half = x.shape[0] // rows
    group = math.gcd(rows, 8)
    cells = group * half
    odd = lax.rem(lax.axis_index("lon"), 2) == 1
    at_north = lax.axis_index("lat") == 0
    at_south = lax.axis_index("lat") == lax.axis_size("lat") - 1
    from_a = col_a[...].astype(F32)
    from_b = col_b[...].astype(F32)
    rims[0] = jnp.where(odd, from_a, from_b)
    rims[1] = jnp.where(odd, from_b, from_a)
    extra[...] = jnp.zeros_like(extra)
    up_acc[...] = jnp.zeros_like(up_acc)
    row_id = lax.broadcasted_iota(jnp.int32, (rows, lanes), 0)
    lane_id = lax.broadcasted_iota(jnp.int32, (rows, lanes), 1)
    top_corner = jnp.logical_and(row_id == 0, lane_id < channels)
    end_corner = jnp.logical_and(row_id == rows - 1, lane_id >= channels)
    for side, d in ((0, 0), (1, 3)):
        lower, upper = rims[side, 0:rows, :], rims[side, 1 : rows + 1, :]
        lower = jnp.where(jnp.logical_and(top_corner, at_north), 0.0, lower)
        upper = jnp.where(jnp.logical_and(end_corner, at_south), 0.0, upper)
        ring = jnp.concatenate([lower, upper], axis=1).astype(BF16)
        rim_feature[side] = product(ring, weights[d], 1, 0)
        rim_conv[side] = product(act_rim[side].astype(BF16), ring, 0, 0)

    def corner(mask, offset, low, high, swap):
        for side, d in ((0, 0), (1, 3)):
            piece = jnp.where(mask, rims[side, offset : offset + rows, :], 0.0)
            blank = jnp.zeros_like(piece)
            parts = [blank, piece] if swap else [piece, blank]
            cap = jnp.concatenate(parts, axis=1).astype(BF16)
            rim_feature[side, :, low:high] += product(cap, weights[d, :, low:high], 1, 0)
            rim_conv[side, low:high, :] += product(
                act_rim[side, :, low:high].astype(BF16), cap, 0, 0
            )

    @pl.when(at_north)
    def _():
        corner(top_corner, 0, 0, lanes, True)

    @pl.when(at_south)
    def _():
        corner(end_corner, 1, lanes, fine, False)

    def step(s, carry):
        start = pl.multiple_of(s * cells, cells)
        for k in range(group):
            at = pl.ds(s * group + k, 1)
            extra[k * half : k * half + 1, :] = rim_feature[0, at, :]
            extra[(k + 1) * half - 1 : (k + 1) * half, :] = rim_feature[1, at, :]
        whole = feature[pl.ds(start, cells), :] + extra[...]
        pre = (whole * slope[pl.ds(start, cells), :]).astype(BF16)
        grad[pl.ds(start, cells), :] = product(pre, up_w[...], 1, 0).astype(BF16)
        up_acc[...] += product(pre, x[pl.ds(start, cells), :], 0, 0)
        return carry

    lax.fori_loop(0, rows // group, step, 0)
    sums[0:fine, :] = up_acc[...]

    def part(d, block):
        at = slice(block * channels, (block + 1) * channels)
        value = conv_acc[d, at, :]
        if d == 0:
            value = value + rim_conv[0, at, :]
        if d == 3:
            value = value + rim_conv[1, at, :]
        return value

    taps = []
    for b in (-1, 0, 1):
        upper = part(1 - b, 0) + part(2 - b, 1)
        lower = part(1 - b, 2) + part(2 - b, 3)
        taps.append(upper + pltpu.roll(lower, fine - channels, 1))
    turned = jnp.concatenate(taps[0:2], axis=0).T
    sums[fine : fine + 3 * channels, :] = turned[0 : 3 * channels]
    turned = jnp.concatenate([taps[2], pltpu.roll(taps[2], fine - channels, 1)], axis=0).T
    sums[fine + 3 * channels : fine + 4 * channels, :] = turned[0:channels]
    sums[fine + 4 * channels : fine + 5 * channels, :] = turned[2 * channels : 3 * channels]


def summed_everywhere(part, scale):
    members = lax.axis_size(AXES)
    rows, lanes = part.shape
    piece = -(-rows // members)
    if members * piece > rows:
        part = jnp.pad(part, ((0, members * piece - rows), (0, 0)))
    parts = lax.all_to_all(part.reshape(members, piece * lanes), AXES, 0, 0, tiled=True)
    own = jnp.sum(parts, axis=0) * scale
    spread = jnp.broadcast_to(own[None], (members, piece * lanes))
    whole = lax.all_to_all(spread, AXES, 0, 0, tiled=True)
    return whole.reshape(members * piece, lanes)[:rows]


def row_routes(lats, lons):
    half = lons // 2
    there = []
    for lat in range(lats):
        for lon in range(lons):
            if lon < half:
                target = (lat + 1, lon) if lat + 1 < lats else (lat, lon + half)
            else:
                target = (lat - 1, lon) if lat > 0 else (lat, lon - half)
            there.append((lat * lons + lon, target[0] * lons + target[1]))
    return there, [(b, a) for a, b in there]


def per_device(coarse_field, cotangent, tconv_weight, conv_weight):
    batch, channels, rows, cols = cotangent.shape
    in_channels = coarse_field.shape[1]
    lats, lons = lax.axis_size("lat"), lax.axis_size("lon")
    assert batch == 1 and lons % 2 == 0
    coarse_rows, half = rows // 2, cols // 2
    cells = coarse_rows * half
    pairs = coarse_rows + 1
    fine = 4 * channels
    lanes = 2 * channels
    scale = 1.0 / math.sqrt(batch * rows * cols * lats * lons)
    group = math.gcd(coarse_rows, 8)

    cot = cotangent.reshape(channels, rows, cols).transpose(1, 0, 2)
    x = coarse_field.transpose(0, 2, 3, 1).reshape(cells, in_channels)
    up_w = tconv_weight.reshape(fine, in_channels)

    first_half = lax.axis_index("lon") < lons // 2
    top, bottom = cot[0], cot[rows - 1]
    there, back = row_routes(lats, lons)
    row_a = lax.ppermute(jnp.where(first_half, bottom, top), AXES, there)
    row_b = lax.ppermute(jnp.where(first_half, top, bottom), AXES, back)

    slope, act_t, act_rim, weights = pl.pallas_call(
        up_kernel,
        out_shape=(
            pltpu.VMEM((cells, fine), F32),
            pltpu.VMEM((fine, cells), BF16),
            pltpu.VMEM((2, coarse_rows, fine), F32),
            pltpu.VMEM((4, fine, fine), BF16),
        ),
        in_specs=[VMEM] * 3,
        out_specs=(VMEM,) * 4,
        scratch_shapes=[pltpu.VMEM((2, channels, 10 * channels), BF16)],
        compiler_params=LIMIT,
        name="up",
    )(x, up_w, conv_weight)
    slope, act_t, act_rim, weights = map(resident, (slope, act_t, act_rim, weights))

    near, polar, send_a, send_b = pl.pallas_call(
        gather_kernel,
        out_shape=(
            pltpu.VMEM((pairs, 4 * half, lanes), BF16),
            pltpu.VMEM((2, 4 * half, lanes), BF16),
            pltpu.VMEM((pairs, lanes), BF16),
            pltpu.VMEM((pairs, lanes), BF16),
        ),
        in_specs=[VMEM] * 4,
        out_specs=(VMEM,) * 4,
        scratch_shapes=[pltpu.VMEM((2, pairs, lanes), F32)],
        compiler_params=LIMIT,
        name="gather",
    )(resident(cot), resident(row_a), resident(row_b), act_rim)

    inner = [(i, i ^ 1) for i in range(lons)]
    outer = [(i, (i + (1 if i % 2 else -1)) % lons) for i in range(lons)]
    col_a = lax.ppermute(send_a, "lon", inner)
    col_b = lax.ppermute(send_b, "lon", outer)

    feature, conv_acc = pl.pallas_call(
        spread_kernel,
        out_shape=(pltpu.VMEM((cells, fine), F32), pltpu.VMEM((4, fine, fine), F32)),
        in_specs=[VMEM] * 4,
        out_specs=(VMEM,) * 2,
        compiler_params=LIMIT,
        name="spread",
    )(resident(near), resident(polar), act_t, weights)

    grad, sums = pl.pallas_call(
        finish_kernel,
        out_shape=(
            jax.ShapeDtypeStruct((cells, in_channels), BF16),
            pltpu.VMEM((fine + 5 * channels, lanes), F32),
        ),
        in_specs=[VMEM] * 9,
        out_specs=(VMEM,) * 2,
        scratch_shapes=[
            pltpu.VMEM((group * half, fine), F32),
            pltpu.VMEM((2, pairs, lanes), F32),
            pltpu.VMEM((2, coarse_rows, fine), F32),
            pltpu.VMEM((2, fine, fine), F32),
            pltpu.VMEM((fine, in_channels), F32),
        ],
        compiler_params=LIMIT,
        name="finish",
    )(
        x, resident(feature), slope, resident(conv_acc), act_rim,
        resident(col_a), resident(col_b), weights, up_w,
    )

    whole = summed_everywhere(sums, scale)
    tconv_grad = whole[:fine].reshape(4, channels, in_channels)
    blocks = whole[fine:].reshape(5, channels, lanes)
    both, last = blocks[3], blocks[4]
    conv_grad = jnp.concatenate(
        [
            blocks[2], last[:, :channels],
            blocks[1], both[:, channels:],
            blocks[0], both[:, :channels],
        ],
        axis=1,
    )
    coarse_grad = grad.reshape(1, coarse_rows, half, in_channels).transpose(0, 3, 1, 2)
    return (coarse_grad, tconv_grad, conv_grad)


def solution(mesh):
    return jax.shard_map(
        per_device,
        mesh=mesh,
        in_specs=(P(None, None, "lat", "lon"), P(None, None, "lat", "lon"), P(), P()),
        out_specs=(P(None, None, "lat", "lon"), P(), P()),
        check_vma=False,
    )
```

time: 66.8 us -> 51.2 us (0.77)
  Pallas kernels: 18.6 us -> 9.64 us
  waiting for transfers between devices: 7.43 us -> 2.73 us
  local copies, waits for them, and re-layouts: 4.61 us -> 3.63 us
    pallas_call x2 -> x4, Pallas kernels: 18.6 us -> 9.64 us  [the longest x1 3.22 us: per_device(): pl.pallas_call(spread_kernel, out_shape=(pltpu.VMEM((cells, fine), F32),...]
    ppermute x1, waiting for transfers between devices: 3.39 us -> 0.01 us  [per_device(): col_b = lax.ppermute(send_b, 'lon', outer)]
    unnamed x15 -> x7, local copies, waits for them, and re-layouts: 3.79 us -> 1.98 us
    ppermute x1, waiting for transfers between devices: 0.84 us -> 0.01 us  [per_device(): row_b = lax.ppermute(jnp.where(first_half, top, bottom), AXES, back)]
    concatenate x1, local copies, waits for them, and re-layouts: 0.01 us -> 0.75 us  [per_device(): jnp.concatenate([blocks[2], last[:, :channels], blocks[1], both[:, channe...]
  transfers between devices with their start and end apart: 4 -> 4, of which waited for: 3 -> 1; matrix products, arithmetic and copies ran while one was open for 1% -> 0% of each run, Pallas kernels for 0% -> 10%
where the time goes in v1:
time: 51.2 us; the launch traced here: 51.1 us
  blocking collectives  28.2 us (55%)
  Pallas kernels  9.64 us (19%)
  starting transfers between devices  5.9 us (12%)
  local copies, waits for them, and re-layouts  3.63 us (7%)
  waiting for transfers between devices  2.73 us (5%)
  between operations  0.75 us (1%)
    all_to_all x1, blocking collectives, summed_everywhere(): lax.all_to_all(part.reshape(members, piece * lanes), AXES, 0, 0, tiled=True)  14.8 us
    all_to_all x1, blocking collectives, summed_everywhere(): whole = lax.all_to_all(spread, AXES, 0, 0, tiled=True)  13.4 us
    ppermute x1, starting transfers between devices, per_device(): row_b = lax.ppermute(jnp.where(first_half, top, bottom), AXES, back)  4.12 us
    pallas_call x1, Pallas kernels, per_device(): pl.pallas_call(spread_kernel, out_shape=(pltpu.VMEM((cells, fine), F32),...  3.22 us
    pallas_call x1, Pallas kernels, per_device(): pl.pallas_call(finish_kernel, out_shape=(jax.ShapeDtypeStruct((cells, in_...  2.86 us
    ppermute x1, waiting for transfers between devices, per_device(): row_a = lax.ppermute(jnp.where(first_half, bottom, top), AXES, there)  2.71 us
    unnamed x7, local copies, waits for them, and re-layouts  1.98 us
    pallas_call x1, Pallas kernels, per_device(): pl.pallas_call(up_kernel, out_shape=(pltpu.VMEM((cells, fine), F32), pltp...  1.89 us
  transfers between devices with their start and end apart: 4, of which 1 were waited for; matrix products, arithmetic and copies ran while one was open for 0% of the time, Pallas kernels for 10%

profile of v1, /device:TPU:0, one launch (start us, length us, event | category | flops | bytes accessed | tf_op | source)
XLA Modules:
  0.0 51.1 jit_solution(15413753122989281796)
XLA Ops:
  0.6 0.0 copy-start.2
  0.6 0.0 copy-start.1
  0.7 0.0 copy-start
  0.7 2.0 %copy.11 = bf16[1,64,64,128]{3,1,2,0:T(8,128)(2,1)S(1)} copy(bf16[1,64,64,128]{3,2,1,0:T(8,128)(2,1)} %param.5) | data formatting | bytes 2097152 | tf_op args[1]
  2.7 4.1 %collective-permute-start.1 = (bf16[64,128]{1,0:T(8,128)(2,1)S(1)}, bf16[64,128]{1,0:T(8,128)(2,1)S(1)}, u32[]{:S(2)}, u32[]{:S(2)}) collective-permute-start(bf16[64,128]{1,0:T(8,128)(2,1)S(1)} %get-tuple-element.27), channel_id=1, source_target_pairs={{8,0},{9,1},{10,2},{11,3},{0,4},{1,5},{2,6},{3,7},{16,8},{17,9},{1... | collective-permute-start | bytes 49160 | tf_op jit(solution)/shard_map/ppermute | solution.py:306
  6.8 0.0 collective-permute-start
  6.8 0.0 copy-done.2
  6.8 0.0 copy-done.1
  6.8 0.0 copy-done
  6.8 1.9 %up.1 = (f32[2048,256]{1,0:T(8,128)S(1)}, bf16[256,2048]{1,0:T(8,128)(2,1)S(1)}, f32[2,32,256]{2,1,0:T(8,128)S(1)}, bf16[4,256,256]{2,1,0:T(8,128)(2,1)S(1)}) custom-call(bf16[2048,128]{1,0:T(8,128)(2,1)S(1)} %bitcast.21, bf16[256,128]{1,0:T(8,128)(2,1)S(1)} %bitcast.24, bf16[64,576]{1,0:T(8,128)(2,1)S(1)} %copy-done.2), custom_call_target="tpu_custom_call" | custom-call | tf_op jit(solution)/shard_map/up/pallas_call | solution.py:308
  8.7 0.0 collective-permute-done.1.recv_b
  8.7 2.7 %collective-permute-done.recv_a = bf16[64,128]{1,0:T(8,128)(2,1)S(1)} collective-permute-done((bf16[64,128]{1,0:T(8,128)(2,1)S(1)}, bf16[64,128]{1,0:T(8,128)(2,1)S(1)}, u32[]{:S(2)}, u32[]{:S(2)}) %collective-permute-start) | collective-permute-done | bytes 16416 | tf_op jit(solution)/shard_map/ppermute | solution.py:305
  11.4 1.7 %gather.1 = (bf16[33,256,128]{2,1,0:T(8,128)(2,1)S(1)}, bf16[2,256,128]{2,1,0:T(8,128)(2,1)S(1)}, bf16[33,128]{1,0:T(8,128)(2,1)S(1)}, bf16[33,128]{1,0:T(8,128)(2,1)S(1)}) custom-call(bf16[64,64,128]{2,1,0:T(8,128)(2,1)S(1)} %bitcast.20, bf16[64,128]{1,0:T(8,128)(2,1)S(1)} %collective-permute-done.recv_a, ...), custom_call_target="tpu_custom_call" | custom-call | tf_op jit(solution)/shard_map/gather/pallas_call | solution.py:324
  13.1 0.1 collective-permute-start.2
  13.2 1.7 %collective-permute-start.3 = (bf16[33,128]{1,0:T(8,128)(2,1)S(1)}, bf16[33,128]{1,0:T(8,128)(2,1)S(1)}, u32[]{:S(2)}, u32[]{:S(2)}) collective-permute-start(bf16[33,128]{1,0:T(8,128)(2,1)S(1)} %get-tuple-element.24), channel_id=1, source_target_pairs={{0,7},{1,2},{2,1},{3,4},{4,3},{5,6},{6,5},{7,0},{8,15},{9,10},{10,... | collective-permute-start | bytes 25352 | tf_op jit(solution)/shard_map/ppermute | solution.py:342
  14.9 3.2 %spread.1 = (f32[2048,256]{1,0:T(8,128)S(1)}, f32[4,256,256]{2,1,0:T(8,128)S(1)}) custom-call(bf16[33,256,128]{2,1,0:T(8,128)(2,1)S(1)} %get-tuple-element.16.near, bf16[2,256,128]{2,1,0:T(8,128)(2,1)S(1)} %get-tuple-element.17.polar, bf16[256,2048]{1,0:T(8,128)(2,1)S(1)} %get-tuple-element.18.act_t, bf16[4,256,256]{2,1,0:T(8,128)(2,1)S(1)} %get-tuple-element.19.weights), custom_call_target="tpu_custom_call" | custom-call | tf_op jit(solution)/shard_map/spread/pallas_call | solution.py:344
  18.1 0.0 collective-permute-done.2.col_a
  18.1 0.0 collective-permute-done.3.col_b
  18.1 2.9 %finish.1 = (bf16[2048,128]{1,0:T(8,128)(2,1)}, f32[576,128]{1,0:T(8,128)S(1)}) custom-call(bf16[2048,128]{1,0:T(8,128)(2,1)S(1)} %bitcast.22, f32[2048,256]{1,0:T(8,128)S(1)} %get-tuple-element.20.feature, f32[2048,256]{1,0:T(8,128)S(1)} %get-tuple-element.21.slope, f32[4,256,256]{2,1,0:T(8,128)S(1)} %get-tuple-element.22.conv_acc, ...), custom_call_target="tpu_custom_call" | custom-call | tf_op jit(solution)/shard_map/finish/pallas_call | solution.py:353
  21.0 14.8 %all_to_all.15 = f32[32,1,2304]{2,1,0:T(1,128)S(1)} all-to-all(f32[32,1,2304]{2,1,0:T(1,128)S(1)} %bitcast.23), channel_id=1, replica_groups=mesh['lat'=4,'lon'=8] {'lat','lon'}, dimensions={0} | all-to-all | bytes 589824 | tf_op jit(solution)/shard_map/all_to_all | solution.py:265
  35.8 0.2 reduce_sum.9
  36.0 0.2 broadcast_in_dim.2
  36.2 13.4 %all_to_all.16 = f32[32,1,2304]{2,1,0:T(1,128)S(1)} all-to-all(f32[32,1,2304]{2,1,0:T(1,128)S(1)} %broadcast_in_dim.2), channel_id=1, replica_groups=mesh['lat'=4,'lon'=8] {'lat','lon'}, dimensions={0} | all-to-all | bytes 589824 | tf_op jit(solution)/shard_map/all_to_all | solution.py:268
  49.6 0.1 fusion
  49.6 0.7 %slice.54 = f32[256,128]{1,0:T(8,128)} slice(f32[576,128]{1,0:T(8,128)S(1)} %bitcast.28), slice={[0:256], [0:128]} | slice | bytes 262144 | tf_op jit(solution)/shard_map/slice | solution.py:376
  50.3 0.7 %concatenate.3 = f32[64,576]{1,0:T(8,128)} concatenate(f32[64,128]{1,0:T(8,128)S(1)} %get-tuple-element.34, f32[64,64]{1,0:T(8,128)S(1)} %get-tuple-element.31, f32[64,128]{1,0:T(8,128)S(1)} %get-tuple-element.33, f32[64,64]{1,0:T(8,128)S(1)} %get-tuple-element.30, f32[64,128]{1,0:T(8,128)S(1)} %get-tuple-element.32, f32[64,64]{1,0:T(8,128)S(1)} %get-tuple-element.29), dimensions={1} | concatenate | bytes 294912 | tf_op jit(solution)/shard_map/concatenate | solution.py:379
  (3 shorter events, 0.0 us)
Async XLA Ops:
  0.6 6.1 %copy-start.2 = (bf16[64,576]{1,0:T(8,128)(2,1)S(1)}, bf16[64,576]{1,0:T(8,128)(2,1)}, u32[]{:S(2)}) copy-start(bf16[64,576]{1,0:T(8,128)(2,1)} %conv_w.1) | copy-start | bytes 221188
  0.6 6.1 %copy-start.1 = (bf16[4,64,128]{2,1,0:T(8,128)(2,1)S(1)}, bf16[4,64,128]{2,1,0:T(8,128)(2,1)}, u32[]{:S(2)}) copy-start(bf16[4,64,128]{2,1,0:T(8,128)(2,1)} %param.6) | copy-start | bytes 196612
  0.7 6.1 %copy-start = (bf16[1,128,32,64]{1,3,2,0:T(8,128)(2,1)S(1)}, bf16[1,128,32,64]{1,3,2,0:T(8,128)(2,1)}, u32[]{:S(2)}) copy-start(bf16[1,128,32,64]{1,3,2,0:T(8,128)(2,1)} %param.4) | copy-start | bytes 1572868
  2.7 6.0 %collective-permute-start.1 = (bf16[64,128]{1,0:T(8,128)(2,1)S(1)}, bf16[64,128]{1,0:T(8,128)(2,1)S(1)}, u32[]{:S(2)}, u32[]{:S(2)}) collective-permute-start(bf16[64,128]{1,0:T(8,128)(2,1)S(1)} %get-tuple-element.27), channel_id=1, source_target_pairs={{8,0},{9,1},{10,2},{11,3},{0,4},{1,5},{2,6},{3,7},{16,8},{17,9},{1... | collective-permute-start | bytes 49160 | tf_op jit(solution)/shard_map/ppermute | solution.py:306
  6.8 4.6 %collective-permute-start = (bf16[64,128]{1,0:T(8,128)(2,1)S(1)}, bf16[64,128]{1,0:T(8,128)(2,1)S(1)}, u32[]{:S(2)}, u32[]{:S(2)}) collective-permute-start(bf16[64,128]{1,0:T(8,128)(2,1)S(1)} %get-tuple-element.28), channel_id=1, source_target_pairs={{0,8},{1,9},{2,10},{3,11},{4,0},{5,1},{6,2},{7,3},{8,16},{9,17},{1... | collective-permute-start | bytes 49160 | tf_op jit(solution)/shard_map/ppermute | solution.py:305
  13.1 5.0 %collective-permute-start.2 = (bf16[33,128]{1,0:T(8,128)(2,1)S(1)}, bf16[33,128]{1,0:T(8,128)(2,1)S(1)}, u32[]{:S(2)}, u32[]{:S(2)}) collective-permute-start(bf16[33,128]{1,0:T(8,128)(2,1)S(1)} %get-tuple-element.23), channel_id=1, source_target_pairs={{0,1},{1,0},{2,3},{3,2},{4,5},{5,4},{6,7},{7,6},{8,9},{9,8},{10,11... | collective-permute-start | bytes 25352 | tf_op jit(solution)/shard_map/ppermute | solution.py:341
  13.2 5.0 %collective-permute-start.3 = (bf16[33,128]{1,0:T(8,128)(2,1)S(1)}, bf16[33,128]{1,0:T(8,128)(2,1)S(1)}, u32[]{:S(2)}, u32[]{:S(2)}) collective-permute-start(bf16[33,128]{1,0:T(8,128)(2,1)S(1)} %get-tuple-element.24), channel_id=1, source_target_pairs={{0,7},{1,2},{2,1},{3,4},{4,3},{5,6},{6,5},{7,0},{8,15},{9,10},{10,... | collective-permute-start | bytes 25352 | tf_op jit(solution)/shard_map/ppermute | solution.py:342

commit v2 on v1

--- a/solution.py
+++ b/solution.py
@@ -233,7 +233,7 @@
         return carry
 
     lax.fori_loop(0, rows // group, step, 0)
-    sums[0:fine, :] = up_acc[...]
+    sums[0:fine, :] = up_acc[...].astype(BF16)
 
     def part(d, block):
         at = slice(block * channels, (block + 1) * channels)
@@ -250,10 +250,24 @@
         lower = part(1 - b, 2) + part(2 - b, 3)
         taps.append(upper + pltpu.roll(lower, fine - channels, 1))
     turned = jnp.concatenate(taps[0:2], axis=0).T
-    sums[fine : fine + 3 * channels, :] = turned[0 : 3 * channels]
+    sums[fine : fine + 3 * channels, :] = turned[0 : 3 * channels].astype(BF16)
     turned = jnp.concatenate([taps[2], pltpu.roll(taps[2], fine - channels, 1)], axis=0).T
-    sums[fine + 3 * channels : fine + 4 * channels, :] = turned[0:channels]
-    sums[fine + 4 * channels : fine + 5 * channels, :] = turned[2 * channels : 3 * channels]
+    sums[fine + 3 * channels : fine + 4 * channels, :] = turned[0:channels].astype(BF16)
+    sums[fine + 4 * channels : fine + 5 * channels, :] = turned[2 * channels : 3 * channels].astype(BF16)
+
+
+def unpack_kernel(whole, tconv_grad, conv_grad):
+    fine, lanes = tconv_grad.shape
+    channels = conv_grad.shape[0]
+    tconv_grad[...] = whole[0:fine].astype(F32)
+    block = [
+        whole[fine + k * channels : fine + (k + 1) * channels].astype(F32) for k in range(5)
+    ]
+    singles = (block[4][:, :channels], block[3][:, channels:], block[3][:, :channels])
+    for a in range(3):
+        start = 3 * a * channels
+        conv_grad[:, start : start + lanes] = block[2 - a]
+        conv_grad[:, start + lanes : start + lanes + channels] = singles[a]
 
 
 def summed_everywhere(part, scale):
@@ -262,9 +276,9 @@
     piece = -(-rows // members)
     if members * piece > rows:
         part = jnp.pad(part, ((0, members * piece - rows), (0, 0)))
-    parts = lax.all_to_all(part.reshape(members, piece * lanes), AXES, 0, 0, tiled=True)
-    own = jnp.sum(parts, axis=0) * scale
-    spread = jnp.broadcast_to(own[None], (members, piece * lanes))
+    parts = lax.all_to_all(part.reshape(members, piece, lanes), AXES, 0, 0, tiled=True)
+    own = (jnp.sum(parts.astype(F32), axis=0) * scale).astype(part.dtype)
+    spread = jnp.broadcast_to(own[None], (members, piece, lanes))
     whole = lax.all_to_all(spread, AXES, 0, 0, tiled=True)
     return whole.reshape(members * piece, lanes)[:rows]
 
@@ -354,7 +368,7 @@
         finish_kernel,
         out_shape=(
             jax.ShapeDtypeStruct((cells, in_channels), BF16),
-            pltpu.VMEM((fine + 5 * channels, lanes), F32),
+            pltpu.VMEM((fine + 5 * channels, lanes), BF16),
         ),
         in_specs=[VMEM] * 9,
         out_specs=(VMEM,) * 2,
@@ -373,17 +387,18 @@
     )
 
     whole = summed_everywhere(sums, scale)
-    tconv_grad = whole[:fine].reshape(4, channels, in_channels)
-    blocks = whole[fine:].reshape(5, channels, lanes)
-    both, last = blocks[3], blocks[4]
-    conv_grad = jnp.concatenate(
-        [
-            blocks[2], last[:, :channels],
-            blocks[1], both[:, channels:],
-            blocks[0], both[:, :channels],
-        ],
-        axis=1,
-    )
+    tconv_grad, conv_grad = pl.pallas_call(
+        unpack_kernel,
+        out_shape=(
+            jax.ShapeDtypeStruct((fine, in_channels), F32),
+            jax.ShapeDtypeStruct((channels, 9 * channels), F32),
+        ),
+        in_specs=[VMEM],
+        out_specs=(VMEM,) * 2,
+        compiler_params=LIMIT,
+        name="unpack",
+    )(resident(whole))
+    tconv_grad = tconv_grad.reshape(4, channels, in_channels)
     coarse_grad = grad.reshape(1, coarse_rows, half, in_channels).transpose(0, 3, 1, 2)
     return (coarse_grad, tconv_grad, conv_grad)
 

time: 51.2 us -> 45.9 us (0.90)
  blocking collectives: 28.2 us -> 23.6 us
  local copies, waits for them, and re-layouts: 3.63 us -> 2.11 us
  Pallas kernels: 9.64 us -> 10.4 us
    all_to_all x1, blocking collectives: 14.8 us -> 12.3 us  [summed_everywhere(): lax.all_to_all(part.reshape(members, piece, lanes), AXES, 0, 0, tiled=True)]
    all_to_all x1, blocking collectives: 13.4 us -> 11.2 us  [summed_everywhere(): whole = lax.all_to_all(spread, AXES, 0, 0, tiled=True)]
    concatenate x1 -> x0, local copies, waits for them, and re-layouts: 0.75 us -> none  [per_device(): jnp.concatenate([blocks[2], last[:, :channels], blocks[1], both[:, channe...]
    slice x3 -> x0, local copies, waits for them, and re-layouts: 0.75 us -> none  [the longest x1 0.66 us: per_device(): tconv_grad = whole[:fine].reshape(4, channels, in_channels)]
    pallas_call x0 -> x1, Pallas kernels: none -> 0.75 us  [per_device(): pl.pallas_call(unpack_kernel, out_shape=(jax.ShapeDtypeStruct((fine, in_c...]
  transfers between devices with their start and end apart: 4 -> 4, of which waited for: 1 -> 1; matrix products, arithmetic and copies ran while one was open for 0% -> 0% of each run, Pallas kernels for 10% -> 11%
where the time goes in v2:
time: 45.9 us; the launch traced here: 45.5 us
  blocking collectives  23.6 us (51%)
  Pallas kernels  10.4 us (23%)
  starting transfers between devices  5.88 us (13%)
  waiting for transfers between devices  2.74 us (6%)
  local copies, waits for them, and re-layouts  2.11 us (5%)
  between operations  0.75 us (2%)
    all_to_all x1, blocking collectives, summed_everywhere(): lax.all_to_all(part.reshape(members, piece, lanes), AXES, 0, 0, tiled=True)  12.3 us
    all_to_all x1, blocking collectives, summed_everywhere(): whole = lax.all_to_all(spread, AXES, 0, 0, tiled=True)  11.2 us
    ppermute x1, starting transfers between devices, per_device(): row_b = lax.ppermute(jnp.where(first_half, top, bottom), AXES, back)  4.12 us
    pallas_call x1, Pallas kernels, per_device(): pl.pallas_call(spread_kernel, out_shape=(pltpu.VMEM((cells, fine), F32),...  3.22 us
    pallas_call x1, Pallas kernels, per_device(): pl.pallas_call(finish_kernel, out_shape=(jax.ShapeDtypeStruct((cells, in_...  2.83 us
    ppermute x1, waiting for transfers between devices, per_device(): row_a = lax.ppermute(jnp.where(first_half, bottom, top), AXES, there)  2.71 us
    unnamed x7, local copies, waits for them, and re-layouts  1.98 us
    pallas_call x1, Pallas kernels, per_device(): pl.pallas_call(up_kernel, out_shape=(pltpu.VMEM((cells, fine), F32), pltp...  1.89 us
  transfers between devices with their start and end apart: 4, of which 1 were waited for; matrix products, arithmetic and copies ran while one was open for 0% of the time, Pallas kernels for 11%

profile of v2, /device:TPU:0, one launch (start us, length us, event | category | flops | bytes accessed | tf_op | source)
XLA Modules:
  0.0 45.5 jit_solution(16603928010092481844)
XLA Ops:
  0.6 0.0 copy-start.2
  0.6 0.0 copy-start.1
  0.7 0.0 copy-start
  0.7 2.0 %copy.10 = bf16[1,64,64,128]{3,1,2,0:T(8,128)(2,1)S(1)} copy(bf16[1,64,64,128]{3,2,1,0:T(8,128)(2,1)} %param.5) | data formatting | bytes 2097152 | tf_op args[1]
  2.7 4.1 %collective-permute-start.1 = (bf16[64,128]{1,0:T(8,128)(2,1)S(1)}, bf16[64,128]{1,0:T(8,128)(2,1)S(1)}, u32[]{:S(2)}, u32[]{:S(2)}) collective-permute-start(bf16[64,128]{1,0:T(8,128)(2,1)S(1)} %get-tuple-element.31), channel_id=1, source_target_pairs={{8,0},{9,1},{10,2},{11,3},{0,4},{1,5},{2,6},{3,7},{16,8},{17,9},{1... | collective-permute-start | bytes 49160 | tf_op jit(solution)/shard_map/ppermute | solution.py:320
  6.8 0.0 collective-permute-start
  6.8 0.0 copy-done.2
  6.8 0.0 copy-done.1
  6.8 0.0 copy-done
  6.8 1.9 %up.1 = (f32[2048,256]{1,0:T(8,128)S(1)}, bf16[256,2048]{1,0:T(8,128)(2,1)S(1)}, f32[2,32,256]{2,1,0:T(8,128)S(1)}, bf16[4,256,256]{2,1,0:T(8,128)(2,1)S(1)}) custom-call(bf16[2048,128]{1,0:T(8,128)(2,1)S(1)} %bitcast.19, bf16[256,128]{1,0:T(8,128)(2,1)S(1)} %bitcast.21, bf16[64,576]{1,0:T(8,128)(2,1)S(1)} %copy-done.2), custom_call_target="tpu_custom_call" | custom-call | tf_op jit(solution)/shard_map/up/pallas_call | solution.py:322
  8.7 0.0 collective-permute-done.1.recv_b
  8.7 2.7 %collective-permute-done.recv_a = bf16[64,128]{1,0:T(8,128)(2,1)S(1)} collective-permute-done((bf16[64,128]{1,0:T(8,128)(2,1)S(1)}, bf16[64,128]{1,0:T(8,128)(2,1)S(1)}, u32[]{:S(2)}, u32[]{:S(2)}) %collective-permute-start) | collective-permute-done | bytes 16416 | tf_op jit(solution)/shard_map/ppermute | solution.py:319
  11.4 1.7 %gather.1 = (bf16[33,256,128]{2,1,0:T(8,128)(2,1)S(1)}, bf16[2,256,128]{2,1,0:T(8,128)(2,1)S(1)}, bf16[33,128]{1,0:T(8,128)(2,1)S(1)}, bf16[33,128]{1,0:T(8,128)(2,1)S(1)}) custom-call(bf16[64,64,128]{2,1,0:T(8,128)(2,1)S(1)} %bitcast.18, bf16[64,128]{1,0:T(8,128)(2,1)S(1)} %collective-permute-done.recv_a, ...), custom_call_target="tpu_custom_call" | custom-call | tf_op jit(solution)/shard_map/gather/pallas_call | solution.py:338
  13.1 0.1 collective-permute-start.2
  13.2 1.7 %collective-permute-start.3 = (bf16[33,128]{1,0:T(8,128)(2,1)S(1)}, bf16[33,128]{1,0:T(8,128)(2,1)S(1)}, u32[]{:S(2)}, u32[]{:S(2)}) collective-permute-start(bf16[33,128]{1,0:T(8,128)(2,1)S(1)} %get-tuple-element.26), channel_id=1, source_target_pairs={{0,7},{1,2},{2,1},{3,4},{4,3},{5,6},{6,5},{7,0},{8,15},{9,10},{10,... | collective-permute-start | bytes 25352 | tf_op jit(solution)/shard_map/ppermute | solution.py:356
  14.9 3.2 %spread.1 = (f32[2048,256]{1,0:T(8,128)S(1)}, f32[4,256,256]{2,1,0:T(8,128)S(1)}) custom-call(bf16[33,256,128]{2,1,0:T(8,128)(2,1)S(1)} %get-tuple-element.18.near, bf16[2,256,128]{2,1,0:T(8,128)(2,1)S(1)} %get-tuple-element.19.polar, bf16[256,2048]{1,0:T(8,128)(2,1)S(1)} %get-tuple-element.20.act_t, bf16[4,256,256]{2,1,0:T(8,128)(2,1)S(1)} %get-tuple-element.21.weights), custom_call_target="tpu_custom_call" | custom-call | tf_op jit(solution)/shard_map/spread/pallas_call | solution.py:358
  18.1 0.0 collective-permute-done.2.col_a
  18.1 0.0 collective-permute-done.3.col_b
  18.1 2.8 %finish.1 = (bf16[2048,128]{1,0:T(8,128)(2,1)}, bf16[576,128]{1,0:T(8,128)(2,1)S(1)}) custom-call(bf16[2048,128]{1,0:T(8,128)(2,1)S(1)} %bitcast.20, f32[2048,256]{1,0:T(8,128)S(1)} %get-tuple-element.22.feature, f32[2048,256]{1,0:T(8,128)S(1)} %get-tuple-element.23.slope, f32[4,256,256]{2,1,0:T(8,128)S(1)} %get-tuple-element.24.conv_acc, ...), custom_call_target="tpu_custom_call" | custom-call | tf_op jit(solution)/shard_map/finish/pallas_call | solution.py:367
  21.0 12.3 %all_to_all.10 = bf16[32,18,128]{2,1,0:T(8,128)(2,1)S(1)} all-to-all(bf16[32,18,128]{2,1,0:T(8,128)(2,1)S(1)} %reshape.39), channel_id=1, replica_groups=mesh['lat'=4,'lon'=8] {'lat','lon'}, dimensions={0} | all-to-all | bytes 294912 | tf_op jit(solution)/shard_map/all_to_all | solution.py:279
  33.4 11.2 %all_to_all.11 = bf16[32,18,128]{2,1,0:T(8,128)(2,1)S(1)} all-to-all(bf16[32,18,128]{2,1,0:T(8,128)(2,1)S(1)} %broadcast_in_dim.2), channel_id=1, replica_groups=mesh['lat'=4,'lon'=8] {'lat','lon'}, dimensions={0} | all-to-all | bytes 294912 | tf_op jit(solution)/shard_map/all_to_all | solution.py:282
  44.7 0.1 reshape.40.whole
  44.7 0.7 %unpack.1 = (f32[256,128]{1,0:T(8,128)}, f32[64,576]{1,0:T(8,128)}) custom-call(bf16[576,128]{1,0:T(8,128)(2,1)S(1)} %reshape.40.whole), custom_call_target="tpu_custom_call" | custom-call | tf_op jit(solution)/shard_map/unpack/pallas_call | solution.py:390
  (5 shorter events, 0.1 us)
Async XLA Ops:
  0.6 6.1 %copy-start.2 = (bf16[64,576]{1,0:T(8,128)(2,1)S(1)}, bf16[64,576]{1,0:T(8,128)(2,1)}, u32[]{:S(2)}) copy-start(bf16[64,576]{1,0:T(8,128)(2,1)} %conv_w.1) | copy-start | bytes 221188
  0.6 6.1 %copy-start.1 = (bf16[4,64,128]{2,1,0:T(8,128)(2,1)S(1)}, bf16[4,64,128]{2,1,0:T(8,128)(2,1)}, u32[]{:S(2)}) copy-start(bf16[4,64,128]{2,1,0:T(8,128)(2,1)} %param.6) | copy-start | bytes 196612
  0.7 6.1 %copy-start = (bf16[1,128,32,64]{1,3,2,0:T(8,128)(2,1)S(1)}, bf16[1,128,32,64]{1,3,2,0:T(8,128)(2,1)}, u32[]{:S(2)}) copy-start(bf16[1,128,32,64]{1,3,2,0:T(8,128)(2,1)} %param.4) | copy-start | bytes 1572868
  2.7 6.0 %collective-permute-start.1 = (bf16[64,128]{1,0:T(8,128)(2,1)S(1)}, bf16[64,128]{1,0:T(8,128)(2,1)S(1)}, u32[]{:S(2)}, u32[]{:S(2)}) collective-permute-start(bf16[64,128]{1,0:T(8,128)(2,1)S(1)} %get-tuple-element.31), channel_id=1, source_target_pairs={{8,0},{9,1},{10,2},{11,3},{0,4},{1,5},{2,6},{3,7},{16,8},{17,9},{1... | collective-permute-start | bytes 49160 | tf_op jit(solution)/shard_map/ppermute | solution.py:320
  6.8 4.6 %collective-permute-start = (bf16[64,128]{1,0:T(8,128)(2,1)S(1)}, bf16[64,128]{1,0:T(8,128)(2,1)S(1)}, u32[]{:S(2)}, u32[]{:S(2)}) collective-permute-start(bf16[64,128]{1,0:T(8,128)(2,1)S(1)} %get-tuple-element.32), channel_id=1, source_target_pairs={{0,8},{1,9},{2,10},{3,11},{4,0},{5,1},{6,2},{7,3},{8,16},{9,17},{1... | collective-permute-start | bytes 49160 | tf_op jit(solution)/shard_map/ppermute | solution.py:319
  13.1 5.0 %collective-permute-start.2 = (bf16[33,128]{1,0:T(8,128)(2,1)S(1)}, bf16[33,128]{1,0:T(8,128)(2,1)S(1)}, u32[]{:S(2)}, u32[]{:S(2)}) collective-permute-start(bf16[33,128]{1,0:T(8,128)(2,1)S(1)} %get-tuple-element.25), channel_id=1, source_target_pairs={{0,1},{1,0},{2,3},{3,2},{4,5},{5,4},{6,7},{7,6},{8,9},{9,8},{10,11... | collective-permute-start | bytes 25352 | tf_op jit(solution)/shard_map/ppermute | solution.py:355
  13.2 5.0 %collective-permute-start.3 = (bf16[33,128]{1,0:T(8,128)(2,1)S(1)}, bf16[33,128]{1,0:T(8,128)(2,1)S(1)}, u32[]{:S(2)}, u32[]{:S(2)}) collective-permute-start(bf16[33,128]{1,0:T(8,128)(2,1)S(1)} %get-tuple-element.26), channel_id=1, source_target_pairs={{0,7},{1,2},{2,1},{3,4},{4,3},{5,6},{6,5},{7,0},{8,15},{9,10},{10,... | collective-permute-start | bytes 25352 | tf_op jit(solution)/shard_map/ppermute | solution.py:356

commit v3 on v2

--- a/solution.py
+++ b/solution.py
@@ -77,103 +77,106 @@
     lax.fori_loop(0, rows // group, step, 0)
 
 
-def gather_kernel(cot, recv_a, recv_b, after, near, polar, send_a, send_b, edges):
+def gather_kernel(cot, after, near, pick, edges):
     rows, channels, cols = cot.shape
     half = cols // 2
     pairs = near.shape[0]
-    first_half = 2 * lax.axis_index("lon") < lax.axis_size("lon")
-    odd = lax.rem(lax.axis_index("lon"), 2) == 1
-    at_north = lax.axis_index("lat") == 0
-    at_south = lax.axis_index("lat") == lax.axis_size("lat") - 1
     row_id = lax.broadcasted_iota(jnp.int32, (4 * half, cols), 0)
     col_id = lax.broadcasted_iota(jnp.int32, (4 * half, cols), 1)
-    pick = jnp.where(col_id == 2 * (row_id % half) + row_id // half - 1, 1.0, 0.0)
-    pick = pick.astype(BF16)
-    from_a = recv_a[...].astype(F32)
-    from_b = recv_b[...].astype(F32)
-    top = jnp.where(first_half, from_a, from_b).astype(BF16)
-    bottom = jnp.where(first_half, from_b, from_a).astype(BF16)
-
-    def keep_edges(m, block):
+    hit = col_id == 2 * (row_id % half) + row_id // half - 1
+    pick[...] = jnp.where(hit, 1.0, 0.0).astype(BF16)
+
+    def emit(m, block):
+        near[m] = block.astype(BF16)
         edges[0, pl.ds(m, 1), :] = block[half : half + 1]
         edges[1, pl.ds(m, 1), :] = block[3 * half - 1 : 3 * half]
 
     def middle(q, carry):
         m = 1 + 2 * q
         four = cot[pl.ds(2 * m - 1, 4)].reshape(4 * channels, cols)
-        out = product(pick, four, 1, 1)
-        for k in range(2):
-            block = out[:, k * 2 * channels : (k + 1) * 2 * channels]
-            near[m + k] = block.astype(BF16)
-            keep_edges(m + k, block)
+        out = product(pick[...], four, 1, 1)
+        emit(m, out[:, : 2 * channels])
+        emit(m + 1, out[:, 2 * channels :])
         return carry
 
-    lane_id = lax.broadcasted_iota(jnp.int32, (4 * half, 2 * channels), 1)
-    ends = ((0, top, cot[0], at_north), (pairs - 1, cot[rows - 1], bottom, at_south))
-    for side, (m, one, two, pole) in enumerate(ends):
-        block = product(pick, jnp.concatenate([one, two], axis=0), 1, 1)
-        keep_edges(m, block)
-        beyond = (lane_id < channels) if side == 0 else (lane_id >= channels)
-        away = jnp.where(jnp.logical_and(beyond, pole), block, 0.0)
-        polar[side] = away.astype(BF16)
-        near[m] = (block - away).astype(BF16)
     lax.fori_loop(0, (pairs - 3) // 2, middle, 0, unroll=3)
+    blank = jnp.zeros((channels, cols), BF16)
+    two = [blank, cot[0], cot[rows - 1], blank]
+    out = product(pick[...], jnp.concatenate(two, axis=0), 1, 1)
+    emit(0, out[:, : 2 * channels])
+    emit(pairs - 1, out[:, 2 * channels :])
     m = pairs - 2
-    block = product(pick, cot[2 * m - 1 : 2 * m + 1].reshape(2 * channels, cols), 1, 1)
-    near[m] = block.astype(BF16)
-    keep_edges(m, block)
-    send_a[...] = jnp.where(odd, edges[0], edges[1]).astype(BF16)
-    send_b[...] = jnp.where(odd, edges[1], edges[0]).astype(BF16)
-
-
-def spread_kernel(near, polar, act_t, weights, feature, conv_acc):
+    emit(m, product(pick[...], cot[2 * m - 1 : 2 * m + 1].reshape(2 * channels, cols), 1, 1))
+
+
+def edge_kernel(recv_a, recv_b, pick, edges, caps, send_a, send_b):
+    quad = caps.shape[1]
+    half, pairs = quad // 4, edges.shape[1]
+    channels = recv_a.shape[0]
+    first_half = 2 * lax.axis_index("lon") < lax.axis_size("lon")
+    odd = lax.rem(lax.axis_index("lon"), 2) == 1
+    from_a = recv_a[...].astype(F32)
+    from_b = recv_b[...].astype(F32)
+    blank = jnp.zeros((channels, recv_a.shape[1]), BF16)
+    top = jnp.where(first_half, from_a, from_b).astype(BF16)
+    bottom = jnp.where(first_half, from_b, from_a).astype(BF16)
+    out = product(pick[...], jnp.concatenate([top, blank, blank, bottom], axis=0), 1, 1)
+    lanes = 2 * channels
+    for side in range(2):
+        caps[side] = out[:, side * lanes : (side + 1) * lanes].astype(BF16)
+    row_id = lax.broadcasted_iota(jnp.int32, (pairs, lanes), 0)
+    rim = []
+    for side, at in ((0, half), (1, 3 * half - 1)):
+        line = out[at : at + 1]
+        rim.append(
+            edges[side]
+            + jnp.where(row_id == 0, line[:, :lanes], 0.0)
+            + jnp.where(row_id == pairs - 1, line[:, lanes:], 0.0)
+        )
+    send_a[...] = jnp.where(odd, rim[0], rim[1]).astype(BF16)
+    send_b[...] = jnp.where(odd, rim[1], rim[0]).astype(BF16)
+
+
+def spread_kernel(near, caps, act_t, weights, feature, conv_acc):
     pairs, quad, lanes = near.shape
     half, rows, fine = quad // 4, pairs - 1, weights.shape[1]
-    group = math.gcd(rows, 8)
-    cells = group * half
+    last = rows * half
+
+    def around(d):
+        piece = slice(d * half, (d + 1) * half)
+        lower = near[0:rows, piece, :].reshape(last, lanes)
+        upper = near[1 : rows + 1, piece, :].reshape(last, lanes)
+        return [lower, upper]
+
+    parts = []
+    for d in range(4):
+        parts += around(d)
     all_w = weights[...].reshape(4 * fine, fine)
-
-    def around(first, count, d):
-        piece = slice(d * half, (d + 1) * half)
-        lower = near[pl.ds(first, count), piece, :].reshape(count * half, lanes)
-        upper = near[pl.ds(first + 1, count), piece, :].reshape(count * half, lanes)
-        return [lower, upper]
-
-    def step(s, carry):
-        parts = []
-        for d in range(4):
-            parts += around(s * group, group, d)
-        start = pl.multiple_of(s * cells, cells)
-        feature[pl.ds(start, cells), :] = product(jnp.concatenate(parts, axis=1), all_w, 1, 0)
-        return carry
-
-    lax.fori_loop(0, rows // group, step, 0)
+    feature[...] = product(jnp.concatenate(parts, axis=1), all_w, 1, 0)
     for d in range(4):
-        conv_acc[d] = product(act_t[...], jnp.concatenate(around(0, rows, d), axis=1), 1, 0)
-
-    @pl.when(lax.axis_index("lat") == 0)
-    def _():
-        for d in range(4):
-            cap = polar[0, d * half : (d + 1) * half, :]
-            feature[0:half, 0:lanes] += product(cap, weights[d, lanes:fine, 0:lanes], 1, 0)
-            conv_acc[d, 0:lanes, lanes:fine] += product(act_t[0:lanes, 0:half], cap, 1, 0)
-
-    @pl.when(lax.axis_index("lat") == lax.axis_size("lat") - 1)
-    def _():
-        last = rows * half
-        for d in range(4):
-            cap = polar[1, d * half : (d + 1) * half, :]
-            feature[last - half : last, lanes:fine] += product(
-                cap, weights[d, 0:lanes, lanes:fine], 1, 0
-            )
-            padded = jnp.concatenate([jnp.zeros_like(cap), cap], axis=0)
-            conv_acc[d, lanes:fine, 0:lanes] += product(
-                act_t[lanes:fine, last - 2 * half : last], padded, 1, 0
-            )
+        conv_acc[d] = product(act_t[...], jnp.concatenate(around(d), axis=1), 1, 0)
+    at_north = lax.axis_index("lat") == 0
+    at_south = lax.axis_index("lat") == lax.axis_size("lat") - 1
+    north = pl.ds(pl.multiple_of(jnp.where(at_north, lanes, 0), lanes), lanes)
+    south = pl.ds(pl.multiple_of(jnp.where(at_south, 0, lanes), lanes), lanes)
+    shape = (half, lanes)
+    total = [jnp.zeros(shape, F32), jnp.zeros(shape, F32)]
+    for d in range(4):
+        top = caps[0, d * half : (d + 1) * half, :]
+        end = caps[1, d * half : (d + 1) * half, :]
+        total[0] += product(top, weights[d, north, 0:lanes], 1, 0)
+        total[1] += product(end, weights[d, south, lanes:fine], 1, 0)
+        conv_acc[d, 0:lanes, north] += product(act_t[0:lanes, 0:half], top, 1, 0)
+        padded = jnp.concatenate([jnp.zeros_like(end), end], axis=0)
+        conv_acc[d, lanes:fine, south] += product(
+            act_t[lanes:fine, last - 2 * half : last], padded, 1, 0
+        )
+    feature[0:half, 0:lanes] += total[0]
+    feature[last - half : last, lanes:fine] += total[1]
 
 
 def finish_kernel(x, feature, slope, conv_acc, act_rim, col_a, col_b, weights, up_w,
-                  grad, sums, extra, rims, rim_feature, rim_conv, up_acc):
+                  grad, sums, rims, rim_feature, rim_conv):
     rows = act_rim.shape[1]
     fine, lanes = weights.shape[1], rims.shape[2]
     channels = lanes // 2
@@ -187,8 +190,6 @@
     from_b = col_b[...].astype(F32)
     rims[0] = jnp.where(odd, from_a, from_b)
     rims[1] = jnp.where(odd, from_b, from_a)
-    extra[...] = jnp.zeros_like(extra)
-    up_acc[...] = jnp.zeros_like(up_acc)
     row_id = lax.broadcasted_iota(jnp.int32, (rows, lanes), 0)
     lane_id = lax.broadcasted_iota(jnp.int32, (rows, lanes), 1)
     top_corner = jnp.logical_and(row_id == 0, lane_id < channels)
@@ -220,20 +221,26 @@
     def _():
         corner(end_corner, 1, lanes, fine, False)
 
-    def step(s, carry):
-        start = pl.multiple_of(s * cells, cells)
-        for k in range(group):
-            at = pl.ds(s * group + k, 1)
-            extra[k * half : k * half + 1, :] = rim_feature[0, at, :]
-            extra[(k + 1) * half - 1 : (k + 1) * half, :] = rim_feature[1, at, :]
-        whole = feature[pl.ds(start, cells), :] + extra[...]
-        pre = (whole * slope[pl.ds(start, cells), :]).astype(BF16)
-        grad[pl.ds(start, cells), :] = product(pre, up_w[...], 1, 0).astype(BF16)
-        up_acc[...] += product(pre, x[pl.ds(start, cells), :], 0, 0)
-        return carry
-
-    lax.fori_loop(0, rows // group, step, 0)
-    sums[0:fine, :] = up_acc[...].astype(BF16)
+    sub_id = lax.broadcasted_iota(jnp.int32, (group, 8, fine), 1)
+    up_grad = None
+    for s in range(rows // group):
+        at = slice(s * cells, (s + 1) * cells)
+        inner = feature[at, :].reshape(group, half, fine)
+        west = rim_feature[0, s * group : (s + 1) * group, :][:, None, :]
+        east = rim_feature[1, s * group : (s + 1) * group, :][:, None, :]
+        whole = jnp.concatenate(
+            [
+                inner[:, 0:8] + jnp.where(sub_id == 0, west, 0.0),
+                inner[:, 8 : half - 8],
+                inner[:, half - 8 :] + jnp.where(sub_id == 7, east, 0.0),
+            ],
+            axis=1,
+        ).reshape(cells, fine)
+        pre = (whole * slope[at, :]).astype(BF16)
+        grad[at, :] = product(pre, up_w[...], 1, 0).astype(BF16)
+        term = product(pre, x[at, :], 0, 0)
+        up_grad = term if up_grad is None else up_grad + term
+    sums[0:fine, :] = up_grad.astype(BF16)
 
     def part(d, block):
         at = slice(block * channels, (block + 1) * channels)
@@ -307,7 +314,6 @@
     fine = 4 * channels
     lanes = 2 * channels
     scale = 1.0 / math.sqrt(batch * rows * cols * lats * lons)
-    group = math.gcd(coarse_rows, 8)
 
     cot = cotangent.reshape(channels, rows, cols).transpose(1, 0, 2)
     x = coarse_field.transpose(0, 2, 3, 1).reshape(cells, in_channels)
@@ -335,20 +341,31 @@
     )(x, up_w, conv_weight)
     slope, act_t, act_rim, weights = map(resident, (slope, act_t, act_rim, weights))
 
-    near, polar, send_a, send_b = pl.pallas_call(
+    near, pick, edges = pl.pallas_call(
         gather_kernel,
         out_shape=(
             pltpu.VMEM((pairs, 4 * half, lanes), BF16),
+            pltpu.VMEM((4 * half, cols), BF16),
+            pltpu.VMEM((2, pairs, lanes), F32),
+        ),
+        in_specs=[VMEM] * 2,
+        out_specs=(VMEM,) * 3,
+        compiler_params=LIMIT,
+        name="gather",
+    )(resident(cot), act_rim)
+
+    caps, send_a, send_b = pl.pallas_call(
+        edge_kernel,
+        out_shape=(
             pltpu.VMEM((2, 4 * half, lanes), BF16),
             pltpu.VMEM((pairs, lanes), BF16),
             pltpu.VMEM((pairs, lanes), BF16),
         ),
         in_specs=[VMEM] * 4,
-        out_specs=(VMEM,) * 4,
-        scratch_shapes=[pltpu.VMEM((2, pairs, lanes), F32)],
-        compiler_params=LIMIT,
-        name="gather",
-    )(resident(cot), resident(row_a), resident(row_b), act_rim)
+        out_specs=(VMEM,) * 3,
+        compiler_params=LIMIT,
+        name="edge",
+    )(resident(row_a), resident(row_b), resident(pick), resident(edges))
 
     inner = [(i, i ^ 1) for i in range(lons)]
     outer = [(i, (i + (1 if i % 2 else -1)) % lons) for i in range(lons)]
@@ -362,7 +379,7 @@
         out_specs=(VMEM,) * 2,
         compiler_params=LIMIT,
         name="spread",
-    )(resident(near), resident(polar), act_t, weights)
+    )(resident(near), resident(caps), act_t, weights)
 
     grad, sums = pl.pallas_call(
         finish_kernel,
@@ -373,11 +390,9 @@
         in_specs=[VMEM] * 9,
         out_specs=(VMEM,) * 2,
         scratch_shapes=[
-            pltpu.VMEM((group * half, fine), F32),
             pltpu.VMEM((2, pairs, lanes), F32),
             pltpu.VMEM((2, coarse_rows, fine), F32),
             pltpu.VMEM((2, fine, fine), F32),
-            pltpu.VMEM((fine, in_channels), F32),
         ],
         compiler_params=LIMIT,
         name="finish",

time: 45.9 us -> 44.1 us (0.961)
  waiting for transfers between devices: 2.74 us -> 1.12 us
  Pallas kernels: 10.4 us -> 8.91 us
  starting transfers between devices: 5.88 us -> 7.12 us
    ppermute x1, waiting for transfers between devices: 2.71 us -> 1.11 us  [per_device(): row_a = lax.ppermute(jnp.where(first_half, bottom, top), AXES, there)]
    ppermute x1, starting transfers between devices: 1.69 us -> 2.93 us  [per_device(): col_b = lax.ppermute(send_b, 'lon', outer)]
    pallas_call x1, Pallas kernels: 2.83 us -> 2 us  [per_device(): pl.pallas_call(finish_kernel, out_shape=(jax.ShapeDtypeStruct((cells, in_...]
    pallas_call x1, Pallas kernels: 3.22 us -> 2.49 us  [per_device(): pl.pallas_call(spread_kernel, out_shape=(pltpu.VMEM((cells, fine), F32),...]
  transfers between devices with their start and end apart: 4 -> 4, of which waited for: 1 -> 1; matrix products, arithmetic and copies ran while one was open for 0% -> 0% of each run, Pallas kernels for 11% -> 14%
where the time goes in v3:
time: 44.1 us; the launch traced here: 43.7 us
  blocking collectives  23.6 us (54%)
  Pallas kernels  8.91 us (20%)
  starting transfers between devices  7.12 us (16%)
  local copies, waits for them, and re-layouts  2.11 us (5%)
  waiting for transfers between devices  1.12 us (3%)
  between operations  0.77 us (2%)
    all_to_all x1, blocking collectives, summed_everywhere(): lax.all_to_all(part.reshape(members, piece, lanes), AXES, 0, 0, tiled=True)  12.3 us
    all_to_all x1, blocking collectives, summed_everywhere(): whole = lax.all_to_all(spread, AXES, 0, 0, tiled=True)  11.2 us
    ppermute x1, starting transfers between devices, per_device(): row_b = lax.ppermute(jnp.where(first_half, top, bottom), AXES, back)  4.12 us
    ppermute x1, starting transfers between devices, per_device(): col_b = lax.ppermute(send_b, 'lon', outer)  2.93 us
    pallas_call x1, Pallas kernels, per_device(): pl.pallas_call(spread_kernel, out_shape=(pltpu.VMEM((cells, fine), F32),...  2.49 us
    pallas_call x1, Pallas kernels, per_device(): pl.pallas_call(finish_kernel, out_shape=(jax.ShapeDtypeStruct((cells, in_...  2 us
    unnamed x7, local copies, waits for them, and re-layouts  1.98 us
    pallas_call x1, Pallas kernels, per_device(): pl.pallas_call(up_kernel, out_shape=(pltpu.VMEM((cells, fine), F32), pltp...  1.89 us
  transfers between devices with their start and end apart: 4, of which 1 were waited for; matrix products, arithmetic and copies ran while one was open for 0% of the time, Pallas kernels for 14%

profile of v3, /device:TPU:0, one launch (start us, length us, event | category | flops | bytes accessed | tf_op | source)
XLA Modules:
  0.0 43.7 jit_solution(9020511404756416101)
XLA Ops:
  0.6 0.0 copy-start.2
  0.6 0.0 copy-start.1
  0.7 0.0 copy-start
  0.7 2.0 %copy.10 = bf16[1,64,64,128]{3,1,2,0:T(8,128)(2,1)S(1)} copy(bf16[1,64,64,128]{3,2,1,0:T(8,128)(2,1)} %param.5) | data formatting | bytes 2097152 | tf_op args[1]
  2.7 4.1 %collective-permute-start.1 = (bf16[64,128]{1,0:T(8,128)(2,1)S(1)}, bf16[64,128]{1,0:T(8,128)(2,1)S(1)}, u32[]{:S(2)}, u32[]{:S(2)}) collective-permute-start(bf16[64,128]{1,0:T(8,128)(2,1)S(1)} %get-tuple-element.35), channel_id=1, source_target_pairs={{8,0},{9,1},{10,2},{11,3},{0,4},{1,5},{2,6},{3,7},{16,8},{17,9},{1... | collective-permute-start | bytes 49160 | tf_op jit(solution)/shard_map/ppermute | solution.py:326
  6.8 0.0 collective-permute-start
  6.8 0.0 copy-done.2
  6.8 0.0 copy-done.1
  6.8 0.0 copy-done
  6.8 1.9 %up.1 = (f32[2048,256]{1,0:T(8,128)S(1)}, bf16[256,2048]{1,0:T(8,128)(2,1)S(1)}, f32[2,32,256]{2,1,0:T(8,128)S(1)}, bf16[4,256,256]{2,1,0:T(8,128)(2,1)S(1)}) custom-call(bf16[2048,128]{1,0:T(8,128)(2,1)S(1)} %bitcast.19, bf16[256,128]{1,0:T(8,128)(2,1)S(1)} %bitcast.21, bf16[64,576]{1,0:T(8,128)(2,1)S(1)} %copy-done.2), custom_call_target="tpu_custom_call" | custom-call | tf_op jit(solution)/shard_map/up/pallas_call | solution.py:328
  8.7 1.6 %gather.1 = (bf16[33,256,128]{2,1,0:T(8,128)(2,1)S(1)}, bf16[256,128]{1,0:T(8,128)(2,1)S(1)}, f32[2,33,128]{2,1,0:T(8,128)S(1)}) custom-call(bf16[64,64,128]{2,1,0:T(8,128)(2,1)S(1)} %bitcast.18, f32[2,32,256]{2,1,0:T(8,128)S(1)} %get-tuple-element.19.after.act_rim), custom_call_target="tpu_custom_call" | custom-call | tf_op jit(solution)/shard_map/gather/pallas_call | solution.py:344
  10.3 0.0 collective-permute-done.1.recv_b
  10.3 1.1 %collective-permute-done.recv_a = bf16[64,128]{1,0:T(8,128)(2,1)S(1)} collective-permute-done((bf16[64,128]{1,0:T(8,128)(2,1)S(1)}, bf16[64,128]{1,0:T(8,128)(2,1)S(1)}, u32[]{:S(2)}, u32[]{:S(2)}) %collective-permute-start) | collective-permute-done | bytes 16416 | tf_op jit(solution)/shard_map/ppermute | solution.py:325
  11.4 0.2 edge.1
  11.6 0.1 collective-permute-start.2
  11.7 2.9 %collective-permute-start.3 = (bf16[33,128]{1,0:T(8,128)(2,1)S(1)}, bf16[33,128]{1,0:T(8,128)(2,1)S(1)}, u32[]{:S(2)}, u32[]{:S(2)}) collective-permute-start(bf16[33,128]{1,0:T(8,128)(2,1)S(1)} %get-tuple-element.30), channel_id=1, source_target_pairs={{0,7},{1,2},{2,1},{3,4},{4,3},{5,6},{6,5},{7,0},{8,15},{9,10},{10,... | collective-permute-start | bytes 25352 | tf_op jit(solution)/shard_map/ppermute | solution.py:373
  14.6 2.5 %spread.1 = (f32[2048,256]{1,0:T(8,128)S(1)}, f32[4,256,256]{2,1,0:T(8,128)S(1)}) custom-call(bf16[33,256,128]{2,1,0:T(8,128)(2,1)S(1)} %get-tuple-element.20.near, bf16[2,256,128]{2,1,0:T(8,128)(2,1)S(1)} %get-tuple-element.23.caps, bf16[256,2048]{1,0:T(8,128)(2,1)S(1)} %get-tuple-element.24.act_t, bf16[4,256,256]{2,1,0:T(8,128)(2,1)S(1)} %get-tuple-element.25.weights), custom_call_target="tpu_custom_call" | custom-call | tf_op jit(solution)/shard_map/spread/pallas_call | solution.py:375
  17.1 0.0 collective-permute-done.2.col_a
  17.1 0.0 collective-permute-done.3.col_b
  17.1 2.0 %finish.1 = (bf16[2048,128]{1,0:T(8,128)(2,1)}, bf16[576,128]{1,0:T(8,128)(2,1)S(1)}) custom-call(bf16[2048,128]{1,0:T(8,128)(2,1)S(1)} %bitcast.20, f32[2048,256]{1,0:T(8,128)S(1)} %get-tuple-element.26.feature, f32[2048,256]{1,0:T(8,128)S(1)} %get-tuple-element.27.slope, f32[4,256,256]{2,1,0:T(8,128)S(1)} %get-tuple-element.28.conv_acc, ...), custom_call_target="tpu_custom_call" | custom-call | tf_op jit(solution)/shard_map/finish/pallas_call | solution.py:384
  19.2 12.3 %all_to_all.10 = bf16[32,18,128]{2,1,0:T(8,128)(2,1)S(1)} all-to-all(bf16[32,18,128]{2,1,0:T(8,128)(2,1)S(1)} %reshape.39), channel_id=1, replica_groups=mesh['lat'=4,'lon'=8] {'lat','lon'}, dimensions={0} | all-to-all | bytes 294912 | tf_op jit(solution)/shard_map/all_to_all | solution.py:286
  31.6 11.2 %all_to_all.11 = bf16[32,18,128]{2,1,0:T(8,128)(2,1)S(1)} all-to-all(bf16[32,18,128]{2,1,0:T(8,128)(2,1)S(1)} %broadcast_in_dim.2), channel_id=1, replica_groups=mesh['lat'=4,'lon'=8] {'lat','lon'}, dimensions={0} | all-to-all | bytes 294912 | tf_op jit(solution)/shard_map/all_to_all | solution.py:289
  42.9 0.1 reshape.40.whole
  42.9 0.7 %unpack.1 = (f32[256,128]{1,0:T(8,128)}, f32[64,576]{1,0:T(8,128)}) custom-call(bf16[576,128]{1,0:T(8,128)(2,1)S(1)} %reshape.40.whole), custom_call_target="tpu_custom_call" | custom-call | tf_op jit(solution)/shard_map/unpack/pallas_call | solution.py:405
  (5 shorter events, 0.1 us)
Async XLA Ops:
  0.6 6.1 %copy-start.2 = (bf16[64,576]{1,0:T(8,128)(2,1)S(1)}, bf16[64,576]{1,0:T(8,128)(2,1)}, u32[]{:S(2)}) copy-start(bf16[64,576]{1,0:T(8,128)(2,1)} %conv_w.1) | copy-start | bytes 221188
  0.6 6.1 %copy-start.1 = (bf16[4,64,128]{2,1,0:T(8,128)(2,1)S(1)}, bf16[4,64,128]{2,1,0:T(8,128)(2,1)}, u32[]{:S(2)}) copy-start(bf16[4,64,128]{2,1,0:T(8,128)(2,1)} %param.6) | copy-start | bytes 196612
  0.7 6.1 %copy-start = (bf16[1,128,32,64]{1,3,2,0:T(8,128)(2,1)S(1)}, bf16[1,128,32,64]{1,3,2,0:T(8,128)(2,1)}, u32[]{:S(2)}) copy-start(bf16[1,128,32,64]{1,3,2,0:T(8,128)(2,1)} %param.4) | copy-start | bytes 1572868
  2.7 7.6 %collective-permute-start.1 = (bf16[64,128]{1,0:T(8,128)(2,1)S(1)}, bf16[64,128]{1,0:T(8,128)(2,1)S(1)}, u32[]{:S(2)}, u32[]{:S(2)}) collective-permute-start(bf16[64,128]{1,0:T(8,128)(2,1)S(1)} %get-tuple-element.35), channel_id=1, source_target_pairs={{8,0},{9,1},{10,2},{11,3},{0,4},{1,5},{2,6},{3,7},{16,8},{17,9},{1... | collective-permute-start | bytes 49160 | tf_op jit(solution)/shard_map/ppermute | solution.py:326
  6.8 4.6 %collective-permute-start = (bf16[64,128]{1,0:T(8,128)(2,1)S(1)}, bf16[64,128]{1,0:T(8,128)(2,1)S(1)}, u32[]{:S(2)}, u32[]{:S(2)}) collective-permute-start(bf16[64,128]{1,0:T(8,128)(2,1)S(1)} %get-tuple-element.36), channel_id=1, source_target_pairs={{0,8},{1,9},{2,10},{3,11},{4,0},{5,1},{6,2},{7,3},{8,16},{9,17},{1... | collective-permute-start | bytes 49160 | tf_op jit(solution)/shard_map/ppermute | solution.py:325
  11.6 5.5 %collective-permute-start.2 = (bf16[33,128]{1,0:T(8,128)(2,1)S(1)}, bf16[33,128]{1,0:T(8,128)(2,1)S(1)}, u32[]{:S(2)}, u32[]{:S(2)}) collective-permute-start(bf16[33,128]{1,0:T(8,128)(2,1)S(1)} %get-tuple-element.29), channel_id=1, source_target_pairs={{0,1},{1,0},{2,3},{3,2},{4,5},{5,4},{6,7},{7,6},{8,9},{9,8},{10,11... | collective-permute-start | bytes 25352 | tf_op jit(solution)/shard_map/ppermute | solution.py:372
  11.7 5.4 %collective-permute-start.3 = (bf16[33,128]{1,0:T(8,128)(2,1)S(1)}, bf16[33,128]{1,0:T(8,128)(2,1)S(1)}, u32[]{:S(2)}, u32[]{:S(2)}) collective-permute-start(bf16[33,128]{1,0:T(8,128)(2,1)S(1)} %get-tuple-element.30), channel_id=1, source_target_pairs={{0,7},{1,2},{2,1},{3,4},{4,3},{5,6},{6,5},{7,0},{8,15},{9,10},{10,... | collective-permute-start | bytes 25352 | tf_op jit(solution)/shard_map/ppermute | solution.py:373

commit v4 on v3

--- a/solution.py
+++ b/solution.py
@@ -6,6 +6,7 @@
 from jax.experimental import pallas as pl
 from jax.experimental.pallas import tpu as pltpu
 from jax.sharding import PartitionSpec as P
+
 
 F32, BF16 = jnp.float32, jnp.bfloat16
 AXES = ("lat", "lon")
@@ -54,7 +55,6 @@
 
 
 def up_kernel(x, up_w, conv_w, slope, act_t, act_rim, weights, packed):
-    fine = up_w.shape[0]
     rows = act_rim.shape[1]
     half = x.shape[0] // rows
     group = math.gcd(rows, 8)
@@ -74,7 +74,7 @@
             act_rim[1, at, :] = active[(k + 1) * half - 1 : (k + 1) * half]
         return carry
 
-    lax.fori_loop(0, rows // group, step, 0)
+    lax.fori_loop(0, rows // group, step, 0, unroll=True)
 
 
 def gather_kernel(cot, after, near, pick, edges):
@@ -99,7 +99,7 @@
         emit(m + 1, out[:, 2 * channels :])
         return carry
 
-    lax.fori_loop(0, (pairs - 3) // 2, middle, 0, unroll=3)
+    lax.fori_loop(0, (pairs - 3) // 2, middle, 0, unroll=5)
     blank = jnp.zeros((channels, cols), BF16)
     two = [blank, cot[0], cot[rows - 1], blank]
     out = product(pick[...], jnp.concatenate(two, axis=0), 1, 1)
@@ -176,12 +176,12 @@
 
 
 def finish_kernel(x, feature, slope, conv_acc, act_rim, col_a, col_b, weights, up_w,
-                  grad, sums, rims, rim_feature, rim_conv):
+                  grad_out, sums, rims, rim_feature, rim_conv, grad, sems):
     rows = act_rim.shape[1]
     fine, lanes = weights.shape[1], rims.shape[2]
     channels = lanes // 2
     half = x.shape[0] // rows
-    group = math.gcd(rows, 8)
+    group = math.gcd(rows, 16)
     cells = group * half
     odd = lax.rem(lax.axis_index("lon"), 2) == 1
     at_north = lax.axis_index("lat") == 0
@@ -223,6 +223,7 @@
 
     sub_id = lax.broadcasted_iota(jnp.int32, (group, 8, fine), 1)
     up_grad = None
+    saves = []
     for s in range(rows // group):
         at = slice(s * cells, (s + 1) * cells)
         inner = feature[at, :].reshape(group, half, fine)
@@ -238,6 +239,8 @@
         ).reshape(cells, fine)
         pre = (whole * slope[at, :]).astype(BF16)
         grad[at, :] = product(pre, up_w[...], 1, 0).astype(BF16)
+        saves.append(pltpu.make_async_copy(grad.at[at], grad_out.at[at], sems.at[s]))
+        saves[s].start()
         term = product(pre, x[at, :], 0, 0)
         up_grad = term if up_grad is None else up_grad + term
     sums[0:fine, :] = up_grad.astype(BF16)
@@ -261,6 +264,8 @@
     turned = jnp.concatenate([taps[2], pltpu.roll(taps[2], fine - channels, 1)], axis=0).T
     sums[fine + 3 * channels : fine + 4 * channels, :] = turned[0:channels].astype(BF16)
     sums[fine + 4 * channels : fine + 5 * channels, :] = turned[2 * channels : 3 * channels].astype(BF16)
+    for save in saves:
+        save.wait()
 
 
 def unpack_kernel(whole, tconv_grad, conv_grad):
@@ -388,11 +393,13 @@
             pltpu.VMEM((fine + 5 * channels, lanes), BF16),
         ),
         in_specs=[VMEM] * 9,
-        out_specs=(VMEM,) * 2,
+        out_specs=(pl.BlockSpec(memory_space=pltpu.HBM), VMEM),
         scratch_shapes=[
             pltpu.VMEM((2, pairs, lanes), F32),
             pltpu.VMEM((2, coarse_rows, fine), F32),
             pltpu.VMEM((2, fine, fine), F32),
+            pltpu.VMEM((cells, in_channels), BF16),
+            pltpu.SemaphoreType.DMA((coarse_rows // math.gcd(coarse_rows, 16),)),
         ],
         compiler_params=LIMIT,
         name="finish",

time: 44.1 us -> 43.3 us (0.982)
  waiting for transfers between devices: 1.12 us -> 2.73 us
  Pallas kernels: 8.91 us -> 7.59 us
  starting transfers between devices: 7.12 us -> 6.08 us
    ppermute x1, waiting for transfers between devices: 1.11 us -> 2.16 us  [per_device(): row_a = lax.ppermute(jnp.where(first_half, bottom, top), AXES, there)]
    ppermute x1, starting transfers between devices: 2.93 us -> 1.89 us  [per_device(): col_b = lax.ppermute(send_b, 'lon', outer)]
    pallas_call x1, Pallas kernels: 1.89 us -> 1.17 us  [per_device(): pl.pallas_call(up_kernel, out_shape=(pltpu.VMEM((cells, fine), F32), pltp...]
    ppermute x1, waiting for transfers between devices: 0.01 us -> 0.56 us  [per_device(): col_b = lax.ppermute(send_b, 'lon', outer)]
  transfers between devices with their start and end apart: 4 -> 4, of which waited for: 1 -> 2; matrix products, arithmetic and copies ran while one was open for 0% -> 0% of each run, Pallas kernels for 14% -> 11%
where the time goes in v4:
time: 43.3 us; the launch traced here: 42.9 us
  blocking collectives  23.6 us (55%)
  Pallas kernels  7.59 us (18%)
  starting transfers between devices  6.08 us (14%)
  waiting for transfers between devices  2.73 us (6%)
  local copies, waits for them, and re-layouts  2.11 us (5%)
  between operations  0.77 us (2%)
    all_to_all x1, blocking collectives, summed_everywhere(): lax.all_to_all(part.reshape(members, piece, lanes), AXES, 0, 0, tiled=True)  12.3 us
    all_to_all x1, blocking collectives, summed_everywhere(): whole = lax.all_to_all(spread, AXES, 0, 0, tiled=True)  11.2 us
    ppermute x1, starting transfers between devices, per_device(): row_b = lax.ppermute(jnp.where(first_half, top, bottom), AXES, back)  4.12 us
    pallas_call x1, Pallas kernels, per_device(): pl.pallas_call(spread_kernel, out_shape=(pltpu.VMEM((cells, fine), F32),...  2.49 us
    ppermute x1, waiting for transfers between devices, per_device(): row_a = lax.ppermute(jnp.where(first_half, bottom, top), AXES, there)  2.16 us
    unnamed x7, local copies, waits for them, and re-layouts  1.98 us
    ppermute x1, starting transfers between devices, per_device(): col_b = lax.ppermute(send_b, 'lon', outer)  1.89 us
    pallas_call x1, Pallas kernels, per_device(): pl.pallas_call(finish_kernel, out_shape=(jax.ShapeDtypeStruct((cells, in_...  1.73 us
  transfers between devices with their start and end apart: 4, of which 2 were waited for; matrix products, arithmetic and copies ran while one was open for 0% of the time, Pallas kernels for 11%

profile of v4, /device:TPU:0, one launch (start us, length us, event | category | flops | bytes accessed | tf_op | source)
XLA Modules:
  0.0 42.9 jit_solution(16511930575122439740)
XLA Ops:
  0.6 0.0 copy-start.2
  0.6 0.0 copy-start.1
  0.7 0.0 copy-start
  0.7 2.0 %copy.10 = bf16[1,64,64,128]{3,1,2,0:T(8,128)(2,1)S(1)} copy(bf16[1,64,64,128]{3,2,1,0:T(8,128)(2,1)} %param.5) | data formatting | bytes 2097152 | tf_op args[1]
  2.7 4.1 %collective-permute-start.1 = (bf16[64,128]{1,0:T(8,128)(2,1)S(1)}, bf16[64,128]{1,0:T(8,128)(2,1)S(1)}, u32[]{:S(2)}, u32[]{:S(2)}) collective-permute-start(bf16[64,128]{1,0:T(8,128)(2,1)S(1)} %get-tuple-element.35), channel_id=1, source_target_pairs={{8,0},{9,1},{10,2},{11,3},{0,4},{1,5},{2,6},{3,7},{16,8},{17,9},{1... | collective-permute-start | bytes 49160 | tf_op jit(solution)/shard_map/ppermute | solution.py:331
  6.8 0.0 collective-permute-start
  6.8 0.0 copy-done.2
  6.8 0.0 copy-done.1
  6.8 0.0 copy-done
  6.8 1.2 %up.1 = (f32[2048,256]{1,0:T(8,128)S(1)}, bf16[256,2048]{1,0:T(8,128)(2,1)S(1)}, f32[2,32,256]{2,1,0:T(8,128)S(1)}, bf16[4,256,256]{2,1,0:T(8,128)(2,1)S(1)}) custom-call(bf16[2048,128]{1,0:T(8,128)(2,1)S(1)} %bitcast.19, bf16[256,128]{1,0:T(8,128)(2,1)S(1)} %bitcast.21, bf16[64,576]{1,0:T(8,128)(2,1)S(1)} %copy-done.2), custom_call_target="tpu_custom_call" | custom-call | tf_op jit(solution)/shard_map/up/pallas_call | solution.py:333
  8.0 1.3 %gather.1 = (bf16[33,256,128]{2,1,0:T(8,128)(2,1)S(1)}, bf16[256,128]{1,0:T(8,128)(2,1)S(1)}, f32[2,33,128]{2,1,0:T(8,128)S(1)}) custom-call(bf16[64,64,128]{2,1,0:T(8,128)(2,1)S(1)} %bitcast.18, f32[2,32,256]{2,1,0:T(8,128)S(1)} %get-tuple-element.19.after.act_rim), custom_call_target="tpu_custom_call" | custom-call | tf_op jit(solution)/shard_map/gather/pallas_call | solution.py:349
  9.2 0.0 collective-permute-done.1.recv_b
  9.3 2.2 %collective-permute-done.recv_a = bf16[64,128]{1,0:T(8,128)(2,1)S(1)} collective-permute-done((bf16[64,128]{1,0:T(8,128)(2,1)S(1)}, bf16[64,128]{1,0:T(8,128)(2,1)S(1)}, u32[]{:S(2)}, u32[]{:S(2)}) %collective-permute-start) | collective-permute-done | bytes 16416 | tf_op jit(solution)/shard_map/ppermute | solution.py:330
  11.4 0.2 edge.1
  11.6 0.1 collective-permute-start.2
  11.7 1.9 %collective-permute-start.3 = (bf16[33,128]{1,0:T(8,128)(2,1)S(1)}, bf16[33,128]{1,0:T(8,128)(2,1)S(1)}, u32[]{:S(2)}, u32[]{:S(2)}) collective-permute-start(bf16[33,128]{1,0:T(8,128)(2,1)S(1)} %get-tuple-element.30), channel_id=1, source_target_pairs={{0,7},{1,2},{2,1},{3,4},{4,3},{5,6},{6,5},{7,0},{8,15},{9,10},{10,... | collective-permute-start | bytes 25352 | tf_op jit(solution)/shard_map/ppermute | solution.py:378
  13.6 2.5 %spread.1 = (f32[2048,256]{1,0:T(8,128)S(1)}, f32[4,256,256]{2,1,0:T(8,128)S(1)}) custom-call(bf16[33,256,128]{2,1,0:T(8,128)(2,1)S(1)} %get-tuple-element.20.near, bf16[2,256,128]{2,1,0:T(8,128)(2,1)S(1)} %get-tuple-element.23.caps, bf16[256,2048]{1,0:T(8,128)(2,1)S(1)} %get-tuple-element.24.act_t, bf16[4,256,256]{2,1,0:T(8,128)(2,1)S(1)} %get-tuple-element.25.weights), custom_call_target="tpu_custom_call" | custom-call | tf_op jit(solution)/shard_map/spread/pallas_call | solution.py:380
  16.1 0.0 collective-permute-done.2.col_a
  16.1 0.6 %collective-permute-done.3.col_b = bf16[33,128]{1,0:T(8,128)(2,1)S(1)} collective-permute-done((bf16[33,128]{1,0:T(8,128)(2,1)S(1)}, bf16[33,128]{1,0:T(8,128)(2,1)S(1)}, u32[]{:S(2)}, u32[]{:S(2)}) %collective-permute-start.3) | collective-permute-done | bytes 8480 | tf_op jit(solution)/shard_map/ppermute | solution.py:378
  16.7 1.7 %finish.1 = (bf16[2048,128]{1,0:T(8,128)(2,1)}, bf16[576,128]{1,0:T(8,128)(2,1)S(1)}) custom-call(bf16[2048,128]{1,0:T(8,128)(2,1)S(1)} %bitcast.20, f32[2048,256]{1,0:T(8,128)S(1)} %get-tuple-element.26.feature, f32[2048,256]{1,0:T(8,128)S(1)} %get-tuple-element.27.slope, f32[4,256,256]{2,1,0:T(8,128)S(1)} %get-tuple-element.28.conv_acc, ...), custom_call_target="tpu_custom_call" | custom-call | tf_op jit(solution)/shard_map/finish/pallas_call | solution.py:389
  18.4 12.3 %all_to_all.10 = bf16[32,18,128]{2,1,0:T(8,128)(2,1)S(1)} all-to-all(bf16[32,18,128]{2,1,0:T(8,128)(2,1)S(1)} %reshape.39), channel_id=1, replica_groups=mesh['lat'=4,'lon'=8] {'lat','lon'}, dimensions={0} | all-to-all | bytes 294912 | tf_op jit(solution)/shard_map/all_to_all | solution.py:291
  30.9 11.2 %all_to_all.11 = bf16[32,18,128]{2,1,0:T(8,128)(2,1)S(1)} all-to-all(bf16[32,18,128]{2,1,0:T(8,128)(2,1)S(1)} %broadcast_in_dim.2), channel_id=1, replica_groups=mesh['lat'=4,'lon'=8] {'lat','lon'}, dimensions={0} | all-to-all | bytes 294912 | tf_op jit(solution)/shard_map/all_to_all | solution.py:294
  42.1 0.1 reshape.40.whole
  42.2 0.7 %unpack.1 = (f32[256,128]{1,0:T(8,128)}, f32[64,576]{1,0:T(8,128)}) custom-call(bf16[576,128]{1,0:T(8,128)(2,1)S(1)} %reshape.40.whole), custom_call_target="tpu_custom_call" | custom-call | tf_op jit(solution)/shard_map/unpack/pallas_call | solution.py:412
  (5 shorter events, 0.1 us)
Async XLA Ops:
  0.6 6.1 %copy-start.2 = (bf16[64,576]{1,0:T(8,128)(2,1)S(1)}, bf16[64,576]{1,0:T(8,128)(2,1)}, u32[]{:S(2)}) copy-start(bf16[64,576]{1,0:T(8,128)(2,1)} %conv_w.1) | copy-start | bytes 221188
  0.6 6.1 %copy-start.1 = (bf16[4,64,128]{2,1,0:T(8,128)(2,1)S(1)}, bf16[4,64,128]{2,1,0:T(8,128)(2,1)}, u32[]{:S(2)}) copy-start(bf16[4,64,128]{2,1,0:T(8,128)(2,1)} %param.6) | copy-start | bytes 196612
  0.7 6.1 %copy-start = (bf16[1,128,32,64]{1,3,2,0:T(8,128)(2,1)S(1)}, bf16[1,128,32,64]{1,3,2,0:T(8,128)(2,1)}, u32[]{:S(2)}) copy-start(bf16[1,128,32,64]{1,3,2,0:T(8,128)(2,1)} %param.4) | copy-start | bytes 1572868
  2.7 6.6 %collective-permute-start.1 = (bf16[64,128]{1,0:T(8,128)(2,1)S(1)}, bf16[64,128]{1,0:T(8,128)(2,1)S(1)}, u32[]{:S(2)}, u32[]{:S(2)}) collective-permute-start(bf16[64,128]{1,0:T(8,128)(2,1)S(1)} %get-tuple-element.35), channel_id=1, source_target_pairs={{8,0},{9,1},{10,2},{11,3},{0,4},{1,5},{2,6},{3,7},{16,8},{17,9},{1... | collective-permute-start | bytes 49160 | tf_op jit(solution)/shard_map/ppermute | solution.py:331
  6.8 4.6 %collective-permute-start = (bf16[64,128]{1,0:T(8,128)(2,1)S(1)}, bf16[64,128]{1,0:T(8,128)(2,1)S(1)}, u32[]{:S(2)}, u32[]{:S(2)}) collective-permute-start(bf16[64,128]{1,0:T(8,128)(2,1)S(1)} %get-tuple-element.36), channel_id=1, source_target_pairs={{0,8},{1,9},{2,10},{3,11},{4,0},{5,1},{6,2},{7,3},{8,16},{9,17},{1... | collective-permute-start | bytes 49160 | tf_op jit(solution)/shard_map/ppermute | solution.py:330
  11.6 4.5 %collective-permute-start.2 = (bf16[33,128]{1,0:T(8,128)(2,1)S(1)}, bf16[33,128]{1,0:T(8,128)(2,1)S(1)}, u32[]{:S(2)}, u32[]{:S(2)}) collective-permute-start(bf16[33,128]{1,0:T(8,128)(2,1)S(1)} %get-tuple-element.29), channel_id=1, source_target_pairs={{0,1},{1,0},{2,3},{3,2},{4,5},{5,4},{6,7},{7,6},{8,9},{9,8},{10,11... | collective-permute-start | bytes 25352 | tf_op jit(solution)/shard_map/ppermute | solution.py:377
  11.7 5.0 %collective-permute-start.3 = (bf16[33,128]{1,0:T(8,128)(2,1)S(1)}, bf16[33,128]{1,0:T(8,128)(2,1)S(1)}, u32[]{:S(2)}, u32[]{:S(2)}) collective-permute-start(bf16[33,128]{1,0:T(8,128)(2,1)S(1)} %get-tuple-element.30), channel_id=1, source_target_pairs={{0,7},{1,2},{2,1},{3,4},{4,3},{5,6},{6,5},{7,0},{8,15},{9,10},{10,... | collective-permute-start | bytes 25352 | tf_op jit(solution)/shard_map/ppermute | solution.py:378
